TPU v7x, 512 devices: a whole 4x8x8 slice. The times are simulated.
512 devices in a mesh: layer: 32 (over z_lo, x, core), dp: 8 (over y), mp: 2 (over z_hi).
Axes of the slice: x: 4, y: 8, z: 8 (z_hi: 2, z_lo: 4; z = z_hi * 4 + z_lo), core: 2. Of those that a mesh axis runs over, the one named last changes fastest.
Arguments:
- states: bfloat16 [128, 1024, 1024], P('layer', 'dp'), may hold values from -6 to 6
- weights: bfloat16 [128, 1024, 1024], P('layer', 'dp', 'mp'), may hold values from -0.1875 to 0.1875
- guess_points: bfloat16 [32, 1024, 1024], P('layer', 'dp'), may hold values from -2 to 2
- cotangent: bfloat16 [1024, 1024], P('dp'), may hold values from -6 to 6
Outputs:
- adjoint: bfloat16 [128, 1024, 1024], P('layer', 'dp', 'mp')
- weight_grads: float32 [128, 1024, 1024], P('layer', 'dp', 'mp')
All inputs are finite; a program needn't handle non-finite values.
Results may differ from a plain program's by a relative error of at most 0.03.
Values may be sent and summed in bfloat16 or wider, within the bound.
No kernel may reach another device: no remote copies, remote signals or barrier semaphores. Data moves between devices by JAX's collectives and lax.ppermute only.
A program may use at most 64 MiB of HBM per device.

v0:
```python
import jax
import jax.numpy as jnp
from jax import lax
from jax.sharding import PartitionSpec as P

step_size = 0.1


def from_behind(value, axis, steps):
    count = lax.axis_size(axis)
    leading, last = (max(0, -steps), min(count, count - steps))
    return lax.ppermute(value, axis, [(source, source + steps) for source in range(leading, last)])


def shortened(array):
    return jax.tree.map(lambda a: a.astype(jnp.bfloat16) if a.dtype == jnp.float32 else a, array)


def slope_of(inputs, weight_block):
    tangent = jnp.tanh(jnp.dot(inputs, weight_block, preferred_element_type=jnp.float32))
    return 1.0 - tangent * tangent


def back_product(scaled_rows, weight_block):
    return lax.dot_general(
        scaled_rows, weight_block, (((1,), (1,)), ((), ())), preferred_element_type=jnp.float32
    )


def body(states, weights, guess_points, cotangent):
    slab_count = lax.axis_size("layer")
    slab_index = lax.axis_index("layer")
    half_index = lax.axis_index("mp")
    layer_count, row_count, model_width = states.shape
    point_count = guess_points.shape[0]
    factor = layer_count // point_count
    columns = weights.shape[2]
    half_rows = row_count // lax.axis_size("mp")
    row_start = half_index * half_rows
    col_start = half_index * columns
    gathered = lax.all_gather(weights, "dp", axis=1, tiled=True)
    next_point = from_behind(guess_points[0], "layer", -1)
    terminal = jnp.where(
        slab_index == slab_count - 1, cotangent.astype(jnp.float32), next_point.astype(jnp.float32)
    )
    guess_wide = guess_points.astype(jnp.float32)
    slopes = [slope_of(states[layer_id], gathered[layer_id]) for layer_id in range(layer_count)]

    def scale_columns(upper_adj, layer_id):
        own_part = lax.dynamic_slice_in_dim(upper_adj, col_start, columns, 1)
        return (own_part * slopes[layer_id]).astype(jnp.bfloat16)

    def fine_step(upper_adj, scaled_rows, layer_id):
        summed = lax.psum(back_product(scaled_rows, gathered[layer_id]), "mp")
        return upper_adj + step_size * summed

    upper_adj = terminal
    residuals = [None] * point_count
    for layer_id in range(layer_count - 1, -1, -1):
        relaxed = fine_step(upper_adj, scale_columns(upper_adj, layer_id), layer_id)
        if layer_id % factor == 0:
            residuals[layer_id // factor] = relaxed - guess_wide[layer_id // factor]
            upper_adj = guess_wide[layer_id // factor]
        else:
            upper_adj = relaxed
    residual_half = lax.dynamic_slice_in_dim(jnp.stack(residuals), row_start, half_rows, 1)
    coarse_weights = lax.all_gather(gathered[::factor], "mp", axis=2, tiled=True)
    state_half = lax.dynamic_slice_in_dim(states[::factor], row_start, half_rows, 1)
    coarse_slopes = jnp.stack([slope_of(state_half[0], coarse_weights[0])])

    def coarse_solve(incoming):
        carried = incoming.astype(jnp.float32)
        results = [None] * point_count
        scaled_rows = (carried * coarse_slopes[0]).astype(jnp.bfloat16)
        stepped = (
            carried
            + factor * step_size * back_product(scaled_rows, coarse_weights[0])
            + residual_half[0]
        )
        results[0] = stepped.astype(jnp.bfloat16)
        return jnp.stack(results)

    def solve_pair(operand_pair):
        return coarse_solve(operand_pair[0])

    def keep_pair(operand_pair):
        return operand_pair[1]

    def one_turn(turn_id, loop_state):
        incoming, errors = loop_state
        errors = lax.cond(
            turn_id == slab_count - 1 - slab_index, solve_pair, keep_pair, (incoming, errors)
        )
        incoming = from_behind(shortened(errors[0]), "layer", -1)
        return (incoming, errors)

    start_in = jnp.zeros((half_rows, model_width), jnp.bfloat16)
    start_errors = jnp.zeros((point_count, half_rows, model_width), jnp.bfloat16)
    incoming, errors = lax.fori_loop(0, slab_count - 1, one_turn, (start_in, start_errors))
    errors = lax.cond(slab_index == 0, solve_pair, keep_pair, (incoming, errors))
    adjoint_parts = [None] * layer_count
    scaled_parts = [None] * layer_count
    spread = lax.all_gather(
        shortened(jnp.concatenate([errors, incoming[None]], 0)), "mp", axis=1, tiled=True
    )
    upper_adj = terminal + spread[point_count].astype(jnp.float32)
    for layer_id in range(layer_count - 1, -1, -1):
        scaled_rows = scale_columns(upper_adj, layer_id)
        if layer_id % factor == 0:
            current = guess_wide[layer_id // factor] + spread[layer_id // factor].astype(
                jnp.float32
            )
        else:
            current = fine_step(upper_adj, scaled_rows, layer_id)
        adjoint_parts[layer_id] = lax.dynamic_slice_in_dim(current, col_start, columns, 1).astype(
            jnp.bfloat16
        )
        scaled_parts[layer_id] = scaled_rows
        upper_adj = current
    adjoint_out = jnp.stack(adjoint_parts)
    scaled_out = jnp.stack(scaled_parts)
    partial_terms = jnp.einsum(
        "lrd,lrh->ldh", states, scaled_out, preferred_element_type=jnp.float32
    )
    weight_grads = step_size * lax.psum_scatter(
        partial_terms.astype(jnp.bfloat16), "dp", scatter_dimension=1, tiled=True
    ).astype(jnp.float32)
    return (adjoint_out, weight_grads)


def solution(mesh):
    return jax.shard_map(
        body,
        mesh=mesh,
        in_specs=(
            P("layer", "dp", None),
            P("layer", "dp", "mp"),
            P("layer", "dp", None),
            P("dp", None),
        ),
        out_specs=(P("layer", "dp", "mp"), P("layer", "dp", "mp")),
        check_vma=False,
    )
```

profile of v0, /device:TPU:1, one launch (start us, length us, event | category | flops | bytes accessed | tf_op | source)
XLA Modules:
  0.0 934.7 jit_solution(8836864910243469288)
XLA Ops:
  8.0 8.7 collective-permute-start.1
  19.1 53.4 %all-gather.3.cloned.1.call-done = bf16[4,1024,512]{2,1,0:T(8,128)(2,1)} async-done(((bf16[4,128,512]{2,1,0:T(8,128)(2,1)}), bf16[4,1024,512]{2,1,0:T(8,128)(2,1)}) %all-gather.3.cloned.1.call-update) | async-done | bytes 4194320 | tf_op jit(solution)/shard_map/all_gather | solution.py:41
  78.4 59.1 %all-reduce.8.cloned.1.call-done = f32[128,1024]{1,0:T(8,128)} async-done(((f32[128,1024]{1,0:T(8,128)}), f32[128,1024]{1,0:T(8,128)}) %all-reduce.8.cloned.1.call-update) | async-done | bytes 524304 | tf_op jit(solution)/shard_map/psum | solution.py:54
  142.7 56.4 %all-reduce.10.cloned.1.call-done = f32[128,1024]{1,0:T(8,128)} async-done(((f32[128,1024]{1,0:T(8,128)}), f32[128,1024]{1,0:T(8,128)}) %all-reduce.10.cloned.1.call-update) | async-done | bytes 524304 | tf_op jit(solution)/shard_map/psum | solution.py:54
  207.4 53.4 %all-reduce.12.cloned.1.call-done = f32[128,1024]{1,0:T(8,128)} async-done(((f32[128,1024]{1,0:T(8,128)}), f32[128,1024]{1,0:T(8,128)}) %all-reduce.12.cloned.1.call-update) | async-done | bytes 524304 | tf_op jit(solution)/shard_map/psum | solution.py:54
  265.6 62.4 %all-gather.5.cloned.1.call-done = bf16[1,1024,1024]{2,1,0:T(8,128)(2,1)} async-done(((bf16[1,1024,512]{2,1,0:T(8,128)(2,1)}), bf16[1,1024,1024]{2,1,0:T(8,128)(2,1)}) %all-gather.5.cloned.1.call-update) | async-done | bytes 2097168 | tf_op jit(solution)/shard_map/all_gather | solution.py:67
  330.0 59.3 %all-reduce.14.cloned.1.call-done = f32[128,1024]{1,0:T(8,128)} async-done(((f32[128,1024]{1,0:T(8,128)}), f32[128,1024]{1,0:T(8,128)}) %all-reduce.14.cloned.1.call-update) | async-done | bytes 524304 | tf_op jit(solution)/shard_map/psum | solution.py:54
  390.3 250.6 %while.23 = (s32[]{:T(128)}, bf16[64,1024]{1,0:T(8,128)(2,1)S(1)}, bf16[1,64,1024]{2,1,0:T(8,128)(2,1)S(1)}, s32[]{:T(128)}, f32[64,1024]{1,0:T(8,128)S(1)}, /*i...) while((s32[]{:T(128)}, bf16[64,1024]{1,0:T(8,128)(2,1)S(1)}, ...), condition=%wide.region_7.8_spmd, body=%wide.region_4.7_spmd.sunk | while | flops 134742016 | bytes 3408051 | solution.py:99
  477.4 6.5 collective-permute-done
  494.2 6.5 collective-permute-done
  502.6 6.5 collective-permute-done
  519.4 6.5 collective-permute-done
  536.1 6.5 collective-permute-done
  552.9 6.5 collective-permute-done
  569.7 6.5 collective-permute-done
  586.5 6.5 collective-permute-done
  603.2 6.5 collective-permute-done
  611.6 20.7 %collective-permute-done = bf16[64,1024]{1,0:T(8,128)(2,1)S(1)} collective-permute-done((bf16[64,1024]{1,0:T(8,128)(2,1)S(1)}, bf16[64,1024]{1,0:T(8,128)(2,1)S(1)}, u32[]{:S(2)}, u32[]{:S(2)}) %collective-permute-start) | collective-permute-done | bytes 131104 | tf_op jit(solution)/shard_map/while/body/eval_jaxpr/ppermute | solution.py:12
  641.0 15.2 %all_gather.11 = bf16[2,128,1024]{2,1,0:T(8,128)(2,1)S(1)} all-gather(bf16[2,64,1024]{2,1,0:T(8,128)(2,1)S(1)} %pad_maximum_fusion.1), channel_id=1, replica_groups=mesh['layer'=32,'dp'=8,'mp'=2] {'mp'}, dimensions={1}, use_global_device_ids=true | all-gather | bytes 786432 | tf_op jit(solution)/shard_map/all_gather | solution.py:103
  658.9 69.1 %all-reduce.16.cloned.1.call-done = f32[128,1024]{1,0:T(8,128)} async-done(((f32[128,1024]{1,0:T(8,128)}), f32[128,1024]{1,0:T(8,128)}) %all-reduce.16.cloned.1.call-update) | async-done | bytes 524304 | tf_op jit(solution)/shard_map/psum | solution.py:54
  731.7 58.0 %all-reduce.18.cloned.1.call-done = f32[128,1024]{1,0:T(8,128)} async-done(((f32[128,1024]{1,0:T(8,128)}), f32[128,1024]{1,0:T(8,128)}) %all-reduce.18.cloned.1.call-update) | async-done | bytes 524304 | tf_op jit(solution)/shard_map/psum | solution.py:54
  793.4 58.0 %all-reduce.20.cloned.1.call-done = f32[128,1024]{1,0:T(8,128)} async-done(((f32[128,1024]{1,0:T(8,128)}), f32[128,1024]{1,0:T(8,128)}) %all-reduce.20.cloned.1.call-update) | async-done | bytes 524304 | tf_op jit(solution)/shard_map/psum | solution.py:54
  856.9 7.8 copy.11
  871.3 53.3 %reduce-scatter.4.cloned.1.call-done = bf16[128,2048]{1,0:T(8,128)(2,1)} async-done(((bf16[1024,2048]{1,0:T(8,128)(2,1)}), bf16[128,2048]{1,0:T(8,128)(2,1)}) %reduce-scatter.4.cloned.1.call-update) | async-done | bytes 524304
  (156 shorter events, 229.3 us)
Async XLA Ops:
  7.2 65.3 %all-gather.3.cloned.1.call-start = ((), (), s32[]{:S(2)}) async-start(), calls=%async_computation.1 | async-start | bytes 4718592 | tf_op jit(solution)/shard_map/all_gather | solution.py:41
  7.9 129.6 %all-reduce.8.cloned.1.call-start = ((), (), s32[]{:S(2)}) async-start(), calls=%async_computation.3 | async-start | bytes 1048576 | tf_op jit(solution)/shard_map/psum | solution.py:54
  8.0 10.1 %collective-permute-start.1 = (bf16[128,1024]{1,0:T(8,128)(2,1)}, bf16[128,1024]{1,0:T(8,128)(2,1)S(1)}, u32[]{:S(2)}, u32[]{:S(2)}) collective-permute-start(bf16[128,1024]{1,0:T(8,128)(2,1)} %bitcast.126), channel_id=1, source_target_pairs={{16,0},{32,16},{48,32},{64,48},{80,64},{96,80},{112,96},{128,112},... | collective-permute-start | bytes 786440 | tf_op jit(solution)/shard_map/ppermute | solution.py:12
  76.8 122.4 %all-reduce.10.cloned.1.call-start = ((), (), s32[]{:S(2)}) async-start(), calls=%async_computation.4 | async-start | bytes 1048576 | tf_op jit(solution)/shard_map/psum | solution.py:54
  141.1 119.7 %all-reduce.12.cloned.1.call-start = ((), (), s32[]{:S(2)}) async-start(), calls=%async_computation.5 | async-start | bytes 1048576 | tf_op jit(solution)/shard_map/psum | solution.py:54
  202.8 125.2 %all-gather.5.cloned.1.call-start = ((), (), s32[]{:S(2)}) async-start(), calls=%async_computation.2 | async-start | bytes 3145728 | tf_op jit(solution)/shard_map/all_gather | solution.py:67
  205.1 184.2 %all-reduce.14.cloned.1.call-start = ((), (), s32[]{:S(2)}) async-start(), calls=%async_computation.6 | async-start | bytes 1048576 | tf_op jit(solution)/shard_map/psum | solution.py:54
  264.5 463.5 %all-reduce.16.cloned.1.call-start = ((), (), s32[]{:S(2)}) async-start(), calls=%async_computation.7 | async-start | bytes 1048576 | tf_op jit(solution)/shard_map/psum | solution.py:54
  467.1 8.4 collective-permute-start
  475.5 8.4 collective-permute-start
  483.9 8.4 collective-permute-start
  492.3 8.4 collective-permute-start
  500.7 8.4 collective-permute-start
  509.1 8.4 collective-permute-start
  517.4 8.4 collective-permute-start
  534.2 8.4 collective-permute-start
  551.0 8.4 collective-permute-start
  567.8 8.4 collective-permute-start
  584.5 8.4 collective-permute-start
  601.3 8.4 collective-permute-start
  609.7 22.6 %collective-permute-start = (bf16[64,1024]{1,0:T(8,128)(2,1)S(1)}, bf16[64,1024]{1,0:T(8,128)(2,1)S(1)}, u32[]{:S(2)}, u32[]{:S(2)}) collective-permute-start(bf16[64,1024]{1,0:T(8,128)(2,1)S(1)} %bitcast.125), channel_id=1, source_target_pairs={{16,0},{32,16},{48,32},{64,48},{80,64},{96,80},{112,96},{128,112},... | collective-permute-start | bytes 393224 | tf_op jit(solution)/shard_map/while/body/eval_jaxpr/ppermute | solution.py:12
  658.9 130.8 %all-reduce.18.cloned.1.call-start = ((), (), s32[]{:S(2)}) async-start(), calls=%async_computation.8 | async-start | bytes 1048576 | tf_op jit(solution)/shard_map/psum | solution.py:54
  731.7 119.7 %all-reduce.20.cloned.1.call-start = ((), (), s32[]{:S(2)}) async-start(), calls=%async_computation.9 | async-start | bytes 1048576 | tf_op jit(solution)/shard_map/psum | solution.py:54
  793.4 131.2 %reduce-scatter.4.cloned.1.call-start = ((), (), s32[]{:S(2)}) async-start(), calls=%async_computation.10 | async-start | bytes 4718592
  (23 other events, 529.6 us)
Sparse Core Ops, SparseCore 0:
  10.1 62.3 all-gather.2
  76.9 60.5 all-reduce.7
  141.2 57.8 all-reduce.9
  202.9 57.8 all-reduce.11
  263.3 64.5 all-gather.4
  331.3 57.9 all-reduce.13
  659.0 68.9 all-reduce.15
  731.8 57.8 all-reduce.17
  793.5 57.8 all-reduce.19
  870.4 54.0 reduce-scatter.3
where the time goes:
time: 937 us; the launch traced here: 935 us
  waiting for transfers between devices  772 us (82%)
  starting transfers between devices  69.2 us (7%)
  matrix products  33.6 us (4%)
  local copies, waits for them, and re-layouts  18.9 us (2%)
  blocking collectives  15.2 us (2%)
  between operations  14.4 us (2%)
  other arithmetic  10.7 us (1%)
    psum x7, waiting for transfers between devices, fine_step(): summed = lax.psum(back_product(scaled_rows, gathered[layer_id]), 'mp')  413 us
    ppermute x32, waiting for transfers between devices, from_behind(): lax.ppermute(value, axis, [(source, source + steps) for source in range(l...  189 us
    ppermute x32, starting transfers between devices, from_behind(): lax.ppermute(value, axis, [(source, source + steps) for source in range(l...  68.8 us
    all_gather x1, waiting for transfers between devices, body(): lax.all_gather(gathered[::factor], 'mp', axis=2, tiled=True)  62.4 us
    unnamed x11, waiting for transfers between devices  54.1 us
    all_gather x1, waiting for transfers between devices, body(): gathered = lax.all_gather(weights, 'dp', axis=1, tiled=True)  53.4 us
    dot_general x8, matrix products, back_product(): lax.dot_general(scaled_rows, weight_block, (((1,), (1,)), ((), ())), pref...  20 us
  transfers between devices with their start and end apart: 42, of which 42 were waited for; matrix products, arithmetic and copies ran while one was open for 2% of the time, Pallas kernels for 0%

commit v1 on v0

v1 whole, which is shorter than its diff:
```python
import functools

import jax
import jax.numpy as jnp
from jax import lax
from jax.experimental import pallas as pl
from jax.experimental.pallas import tpu as pltpu
from jax.sharding import Mesh
from jax.sharding import PartitionSpec as P

step_size = 0.1
BF = jnp.bfloat16
F32 = jnp.float32
LAYER = ("zl", "x", "core")
RING = ("x", "core")


def back_product(scaled, weight):
    return lax.dot_general(scaled, weight, (((1,), (1,)), ((), ())), preferred_element_type=F32)


def swapped(value, axis):
    return lax.ppermute(value, axis, [(0, 1), (1, 0)])


def rotated(value, axis, steps):
    count = lax.axis_size(axis)
    return lax.ppermute(value, axis, [(i, (i + steps) % count) for i in range(count)])


def relax_kernel(blocks, states_ref, rest_ref, coarse_ref, term_ref, guess_ref, slopes_ref, pack_ref, v_ref):
    turn = pl.program_id(0)
    last = pl.num_programs(0) - 1
    rows, width = v_ref.shape

    @pl.when(turn == 0)
    def _():
        v_ref[...] = term_ref[...].astype(F32)

    def step(weight):
        tangent = jnp.tanh(jnp.dot(states_ref[0], weight, preferred_element_type=F32))
        slope = 1.0 - tangent * tangent
        slopes_ref[0] = slope
        scaled = (v_ref[...] * slope).astype(BF)
        return v_ref[...] + step_size * back_product(scaled, weight), slope

    @pl.when(turn < last)
    def _():
        v_ref[...] = step(rest_ref[0])[0]

    @pl.when(turn == last)
    def _():
        relaxed, slope = step(coarse_ref[...])
        residual = relaxed - guess_ref[...].astype(F32)
        part = rows // blocks
        pack_ref[:, :part, :] = residual.astype(BF).reshape(blocks, part, width)
        pack_ref[:, part:, :] = slope.astype(BF).reshape(blocks, part, width)


def relax(states, rest, coarse, terminal, guess, blocks):
    layers, rows, width = states.shape
    top = layers - 1
    return pl.pallas_call(
        functools.partial(relax_kernel, blocks),
        grid=(layers,),
        in_specs=[
            pl.BlockSpec((1, rows, width), lambda t: (top - t, 0, 0)),
            pl.BlockSpec((1, width, width), lambda t: (jnp.maximum(top - 1 - t, 0), 0, 0)),
            pl.BlockSpec((width, width), lambda t: (0, 0)),
            pl.BlockSpec((rows, width), lambda t: (0, 0)),
            pl.BlockSpec((rows, width), lambda t: (0, 0)),
        ],
        out_specs=[
            pl.BlockSpec((1, rows, width), lambda t: (top - t, 0, 0)),
            pl.BlockSpec((blocks, 2 * rows // blocks, width), lambda t: (0, 0, 0)),
        ],
        out_shape=[
            jax.ShapeDtypeStruct((layers, rows, width), F32),
            jax.ShapeDtypeStruct((blocks, 2 * rows // blocks, width), BF),
        ],
        scratch_shapes=[pltpu.VMEM((rows, width), F32)],
        compiler_params=pltpu.CompilerParams(vmem_limit_bytes=40 * 2**20),
        name="relax",
    )(states, rest, coarse, terminal, guess)


def chain_kernel(count, place_ref, pack_ref, own_ref, other_ref, in_ref, out_ref, low_ref, v_ref):
    turn = pl.program_id(0)
    part = in_ref.shape[0]
    scale = 4 * step_size
    chip = count - 1 - turn

    @pl.when(turn == 0)
    def _():
        v_ref[...] = in_ref[...].astype(F32)

    def two(high, low):
        v = v_ref[...]
        for side, weight in ((1, high), (0, low)):
            point = 2 * chip + side
            scaled = (v * pack_ref[point, part:, :].astype(F32)).astype(BF)
            out_ref[point, :part, :] = v.astype(BF)
            residual = pack_ref[point, :part, :].astype(F32)
            short = (v + scale * back_product(scaled, weight[0]) + residual).astype(BF)
            out_ref[point, part:, :] = short
            v = short.astype(F32)
        v_ref[...] = v
        low_ref[...] = v.astype(BF)

    @pl.when(place_ref[1] == 1)
    def _():
        two(own_ref, other_ref)

    @pl.when(place_ref[1] == 0)
    def _():
        two(other_ref, own_ref)


def chain(place, pack, own, other, incoming):
    count, width = own.shape[0], own.shape[1]
    part = incoming.shape[0]
    weight_spec = pl.BlockSpec((1, width, width), lambda t, place: ((2 * count - 1 - t - place[0]) % count, 0, 0))
    return pl.pallas_call(
        functools.partial(chain_kernel, count),
        grid_spec=pltpu.PrefetchScalarGridSpec(
            num_scalar_prefetch=1,
            grid=(count,),
            in_specs=[
                pl.BlockSpec((2 * count, 2 * part, width), lambda t, place: (0, 0, 0)),
                weight_spec,
                weight_spec,
                pl.BlockSpec((part, width), lambda t, place: (0, 0)),
            ],
            out_specs=[
                pl.BlockSpec((2 * count, 2 * part, width), lambda t, place: (0, 0, 0)),
                pl.BlockSpec((part, width), lambda t, place: (0, 0)),
            ],
            scratch_shapes=[pltpu.VMEM((part, width), F32)],
        ),
        out_shape=[
            jax.ShapeDtypeStruct((2 * count, 2 * part, width), BF),
            jax.ShapeDtypeStruct((part, width), BF),
        ],
        compiler_params=pltpu.CompilerParams(vmem_limit_bytes=40 * 2**20),
        name="chain",
    )(place, pack, own, other, incoming)


def correct_kernel(place_ref, spread_ref, states_ref, slopes_ref, rest_ref, term_ref, guess_ref, adj_ref, part_ref, v_ref):
    turn = pl.program_id(0)
    last = pl.num_programs(0) - 1
    rows, width = v_ref.shape
    half = width // 2
    part = spread_ref.shape[1] // 2

    def own_half(value):
        return jnp.where(place_ref[2] == 0, value[:, :half], value[:, half:])

    @pl.when(turn == 0)
    def _():
        error = spread_ref[:, :part, :].reshape(rows, width)
        v_ref[...] = term_ref[...].astype(F32) + error.astype(F32)

    scaled = (v_ref[...] * slopes_ref[0]).astype(BF)
    terms = lax.dot_general(
        states_ref[0], own_half(scaled), (((0,), (0,)), ((), ())), preferred_element_type=F32
    )
    part_ref[0] = terms.astype(BF)

    @pl.when(turn < last)
    def _():
        current = v_ref[...] + step_size * back_product(scaled, rest_ref[0])
        v_ref[...] = current
        adj_ref[0] = own_half(current).astype(BF)

    @pl.when(turn == last)
    def _():
        error = spread_ref[:, part:, :].reshape(rows, width)
        adj_ref[0] = own_half(guess_ref[...].astype(F32) + error.astype(F32)).astype(BF)


def correct(place, spread, states, slopes, rest, terminal, guess):
    layers, rows, width = states.shape
    half = width // 2
    top = layers - 1
    return pl.pallas_call(
        correct_kernel,
        grid_spec=pltpu.PrefetchScalarGridSpec(
            num_scalar_prefetch=1,
            grid=(layers,),
            in_specs=[
                pl.BlockSpec(spread.shape, lambda t, place: (0, 0, 0)),
                pl.BlockSpec((1, rows, width), lambda t, place: (top - t, 0, 0)),
                pl.BlockSpec((1, rows, width), lambda t, place: (top - t, 0, 0)),
                pl.BlockSpec((1, width, width), lambda t, place: (jnp.maximum(top - 1 - t, 0), 0, 0)),
                pl.BlockSpec((rows, width), lambda t, place: (0, 0)),
                pl.BlockSpec((rows, width), lambda t, place: (0, 0)),
            ],
            out_specs=[
                pl.BlockSpec((1, rows, half), lambda t, place: (top - t, 0, 0)),
                pl.BlockSpec((1, width, half), lambda t, place: (top - t, 0, 0)),
            ],
            scratch_shapes=[pltpu.VMEM((rows, width), F32)],
        ),
        out_shape=[
            jax.ShapeDtypeStruct((layers, rows, half), BF),
            jax.ShapeDtypeStruct((layers, width, half), BF),
        ],
        compiler_params=pltpu.CompilerParams(vmem_limit_bytes=40 * 2**20),
        name="correct",
    )(place, spread, states, slopes, rest, terminal, guess)


def body(states, weights, guess_points, cotangent):
    slabs = lax.axis_size(LAYER)
    slab = lax.axis_index(LAYER)
    half_index = lax.axis_index("mp")
    place = jnp.stack([lax.axis_index("x"), lax.axis_index("core"), half_index]).astype(jnp.int32)
    blocks = lax.axis_size(RING)
    width = states.shape[2]
    mid = width // 2
    guess = guess_points[0]

    def whole_rows(own):
        other = swapped(own, "mp")
        return jnp.where(
            half_index == 0,
            jnp.concatenate([own, other], -1),
            jnp.concatenate([other, own], -1),
        )

    next_guess = lax.ppermute(guess, LAYER, [(i, i - 1) for i in range(1, slabs)])
    terminal = jnp.where(slab == slabs - 1, cotangent, next_guess)
    coarse = lax.all_gather(whole_rows(weights[0]), "dp", axis=0, tiled=True)
    rest = lax.all_gather(whole_rows(weights[1:]), "dp", axis=1, tiled=True)

    ahead = rotated(coarse, "x", -1)
    behind = rotated(coarse, "x", 1)
    across = jnp.concatenate([rotated(ahead[:mid], "x", -1), rotated(behind[mid:], "x", 1)], 0)
    own = jnp.stack([coarse, ahead, across, behind])
    other = swapped(own, "core")

    slopes, pack = relax(states, rest, coarse, terminal, guess, blocks)
    pack = lax.all_to_all(pack, RING, 0, 0, tiled=True)

    incoming = jnp.zeros((pack.shape[1] // 2, width), BF)
    stages = lax.axis_size("zl")
    for stage in range(stages):
        errors, lowest = chain(place, pack, own, other, incoming)
        if stage < stages - 1:
            incoming = lax.ppermute(lowest, "zl", [(i, i - 1) for i in range(1, stages)])
    spread = lax.all_to_all(errors, RING, 0, 0, tiled=True)

    adjoint, partial = correct(place, spread, states, slopes, rest, terminal, guess)
    grads = lax.psum_scatter(partial, "dp", scatter_dimension=1, tiled=True)
    return adjoint, step_size * grads.astype(F32)


def solution(mesh):
    slabs, rows, halves = (mesh.shape[name] for name in ("layer", "dp", "mp"))
    fine = Mesh(
        mesh.devices.reshape(slabs // 8, 4, 2, rows, halves), ("zl", "x", "core", "dp", "mp")
    )
    return jax.shard_map(
        body,
        mesh=fine,
        in_specs=(
            P(LAYER, "dp", None),
            P(LAYER, "dp", "mp"),
            P(LAYER, "dp", None),
            P("dp", None),
        ),
        out_specs=(P(LAYER, "dp", "mp"), P(LAYER, "dp", "mp")),
        check_vma=False,
    )
```

time: 937 us -> 344 us (0.37)
  waiting for transfers between devices: 772 us -> 187 us
  Pallas kernels: 0 us -> 50.8 us
  matrix products: 33.6 us -> 0 us
  starting transfers between devices: 69.2 us -> 52.2 us
    psum x7 -> x0, waiting for transfers between devices: 413 us -> none  [fine_step(): summed = lax.psum(back_product(scaled_rows, gathered[layer_id]), 'mp')]
    ppermute x32 -> x11, waiting for transfers between devices: 189 us -> 71.3 us  [the longest x4 38.6 us: rotated(): lax.ppermute(value, axis, [(i, (i + steps) % count) for i in range(count)])]
    all_gather x2, waiting for transfers between devices: 116 us -> 51.5 us  [the longest x1 43.2 us: body(): coarse = lax.all_gather(whole_rows(weights[0]), 'dp', axis=0, tiled=True)]
    reduce_scatter x0 -> x1, waiting for transfers between devices: none -> 55.3 us  [body(): grads = lax.psum_scatter(partial, 'dp', scatter_dimension=1, tiled=True)]
    unnamed x11 -> x3, waiting for transfers between devices: 54.1 us -> 0.05 us
    pallas_call x0 -> x6, Pallas kernels: none -> 50.8 us  [the longest x4 38.6 us: chain(): pl.pallas_call(functools.partial(chain_kernel, count), grid_spec=pltpu.Pr...]
    dot_general x14 -> x0, matrix products: 33.6 us -> none  [the longest x8 20 us: back_product(): lax.dot_general(scaled_rows, weight_block, (((1,), (1,)), ((), ())), pref...]
    ppermute x32 -> x11, starting transfers between devices: 68.8 us -> 47 us  [the longest x3 27.9 us: swapped(): return lax.ppermute(value, axis, [(0, 1), (1, 0)])]
  transfers between devices with their start and end apart: 42 -> 15, of which waited for: 42 -> 13; matrix products, arithmetic and copies ran while one was open for 2% -> 3% of each run, Pallas kernels for 0% -> 1%
where the time goes in v1:
time: 344 us; the launch traced here: 343 us
  waiting for transfers between devices  187 us (54%)
  starting transfers between devices  52.2 us (15%)
  Pallas kernels  50.8 us (15%)
  blocking collectives  16.1 us (5%)
  between operations  14 us (4%)
  local copies, waits for them, and re-layouts  11.2 us (3%)
  other arithmetic  11.1 us (3%)
    reduce_scatter x1, waiting for transfers between devices, body(): grads = lax.psum_scatter(partial, 'dp', scatter_dimension=1, tiled=True)  55.3 us
    all_gather x1, waiting for transfers between devices, body(): coarse = lax.all_gather(whole_rows(weights[0]), 'dp', axis=0, tiled=True)  43.2 us
    ppermute x4, waiting for transfers between devices, rotated(): lax.ppermute(value, axis, [(i, (i + steps) % count) for i in range(count)])  38.6 us
    pallas_call x4, Pallas kernels, chain(): pl.pallas_call(functools.partial(chain_kernel, count), grid_spec=pltpu.Pr...  38.6 us
    ppermute x3, starting transfers between devices, swapped(): return lax.ppermute(value, axis, [(0, 1), (1, 0)])  27.9 us
    all_to_all x1, blocking collectives, body(): spread = lax.all_to_all(errors, RING, 0, 0, tiled=True)  16.1 us
    ppermute x4, starting transfers between devices, rotated(): lax.ppermute(value, axis, [(i, (i + steps) % count) for i in range(count)])  13.2 us
    ppermute x1, waiting for transfers between devices, body(): lax.ppermute(guess, LAYER, [(i, i - 1) for i in range(1, slabs)])  11.5 us
  transfers between devices with their start and end apart: 15, of which 13 were waited for; matrix products, arithmetic and copies ran while one was open for 3% of the time, Pallas kernels for 1%

profile of v1, /device:TPU:1, one launch (start us, length us, event | category | flops | bytes accessed | tf_op | source)
XLA Modules:
  0.0 342.9 jit_solution(8084151485260675470)
XLA Ops:
  8.1 11.5 %collective-permute-start.1 = (bf16[128,512]{1,0:T(8,128)(2,1)S(1)}, bf16[128,512]{1,0:T(8,128)(2,1)S(1)}, u32[]{:S(2)}, u32[]{:S(2)}) collective-permute-start(bf16[128,512]{1,0:T(8,128)(2,1)S(1)} %slice_bitcast_fusion), channel_id=1, source_target_pairs={{0,1},{1,0},{2,3},{3,2},{4,5},{5,4},{6,7},{7,6},{8,9},{9,8},{10,11... | collective-permute-start | bytes 393224 | tf_op jit(solution)/shard_map/ppermute | solution.py:23
  19.6 3.9 %collective-permute-done.1 = bf16[128,512]{1,0:T(8,128)(2,1)S(1)} collective-permute-done((bf16[128,512]{1,0:T(8,128)(2,1)S(1)}, bf16[128,512]{1,0:T(8,128)(2,1)S(1)}, u32[]{:S(2)}, u32[]{:S(2)}) %collective-permute-start.1) | collective-permute-done | bytes 131104 | tf_op jit(solution)/shard_map/ppermute | solution.py:23
  24.3 43.2 %all-gather.5.cloned.1.call-done.coarse_ref = bf16[1024,1024]{1,0:T(8,128)(2,1)} async-done(((bf16[128,1024]{1,0:T(8,128)(2,1)}), bf16[1024,1024]{1,0:T(8,128)(2,1)}) %all-gather.5.cloned.1.call-update) | async-done | bytes 2097168 | tf_op jit(solution)/shard_map/all_gather | solution.py:234
  70.7 3.4 collective-permute-start.3
  75.1 7.7 %collective-permute-start = (bf16[3,128,512]{2,1,0:T(8,128)(2,1)S(1)}, bf16[3,128,512]{2,1,0:T(8,128)(2,1)S(1)}, u32[]{:S(2)}, u32[]{:S(2)}) collective-permute-start(bf16[3,128,512]{2,1,0:T(8,128)(2,1)S(1)} %slice.12), channel_id=1, source_target_pairs={{0,1},{1,0},{2,3},{3,2},{4,5},{5,4},{6,7},{7,6},{8,9},{9,8},{10,11... | collective-permute-start | bytes 1179656 | tf_op jit(solution)/shard_map/ppermute | solution.py:23
  82.8 7.2 %collective-permute-done = bf16[3,128,512]{2,1,0:T(8,128)(2,1)S(1)} collective-permute-done((bf16[3,128,512]{2,1,0:T(8,128)(2,1)S(1)}, bf16[3,128,512]{2,1,0:T(8,128)(2,1)S(1)}, u32[]{:S(2)}, u32[]{:S(2)}) %collective-permute-start) | collective-permute-done | bytes 393248 | tf_op jit(solution)/shard_map/ppermute | solution.py:23
  91.1 22.1 %collective-permute-done.5 = bf16[1024,1024]{1,0:T(8,128)(2,1)S(1)} collective-permute-done((bf16[1024,1024]{1,0:T(8,128)(2,1)}, bf16[1024,1024]{1,0:T(8,128)(2,1)S(1)}, u32[]{:S(2)}, u32[]{:S(2)}) %collective-permute-start.5) | collective-permute-done | bytes 2097184 | tf_op jit(solution)/shard_map/ppermute | solution.py:28
  116.6 4.8 %collective-permute-start.4 = (bf16[512,1024]{1,0:T(8,128)(2,1)S(1)}, bf16[512,1024]{1,0:T(8,128)(2,1)S(1)}, u32[]{:S(2)}, u32[]{:S(2)}) collective-permute-start(bf16[512,1024]{1,0:T(8,128)(2,1)S(1)} %slice.16), channel_id=1, source_target_pairs={{0,96},{32,0},{64,32},{96,64},{1,97},{33,1},{65,33},{97,65},{2,98}... | collective-permute-start | bytes 3145736 | tf_op jit(solution)/shard_map/ppermute | solution.py:28
  121.4 14.1 %collective-permute-done.6 = bf16[512,1024]{1,0:T(8,128)(2,1)S(1)} collective-permute-done((bf16[512,1024]{1,0:T(8,128)(2,1)S(1)}, bf16[512,1024]{1,0:T(8,128)(2,1)S(1)}, u32[]{:S(2)}, u32[]{:S(2)}) %collective-permute-start.6) | collective-permute-done | bytes 1048608 | tf_op jit(solution)/shard_map/ppermute | solution.py:28
  138.2 5.9 %pad_maximum_fusion.own_ref = bf16[4,1024,1024]{2,1,0:T(8,128)(2,1)} fusion(bf16[1,1024,1024]{2,1,0:T(8,128)(2,1)S(1)} %bitcast.15, bf16[1,1024,1024]{2,1,0:T(8,128)(2,1)S(1)} %maximum_bitcast_fusion, bf16[1,1024,1024]{2,1,0:T(8,128)(2,1)} %bitcast.6, bf16[1,1024,1024]{2,1,0:T(8,128)(2,1)S(1)} %bitcast.11), kind=kLoop, calls=%fused_computation | loop fusion | flops 12582912 | bytes 16777216 | tf_op jit(solution)/shard_map/stack | solution.py:240
  144.0 8.7 %collective-permute-start.7 = (bf16[4,1024,1024]{2,1,0:T(8,128)(2,1)}, bf16[4,1024,1024]{2,1,0:T(8,128)(2,1)}, u32[]{:S(2)}, u32[]{:S(2)}) collective-permute-start(bf16[4,1024,1024]{2,1,0:T(8,128)(2,1)} %pad_maximum_fusion.own_ref), channel_id=1, source_target_pairs={{0,16},{16,0},{1,17},{17,1},{2,18},{18,2},{3,19},{19,3},{4,20},{20... | collective-permute-start | bytes 25165832 | tf_op jit(solution)/shard_map/ppermute | solution.py:23
  154.7 11.5 %collective-permute-done.2 = bf16[128,1024]{1,0:T(8,128)(2,1)} collective-permute-done((bf16[128,1024]{1,0:T(8,128)(2,1)S(1)}, bf16[128,1024]{1,0:T(8,128)(2,1)}, u32[]{:S(2)}, u32[]{:S(2)}) %collective-permute-start.2) | collective-permute-done | bytes 262176 | tf_op jit(solution)/shard_map/ppermute | solution.py:232
  167.2 8.3 %all-gather.3.cloned.1.call-done.rest_ref = bf16[3,1024,1024]{2,1,0:T(8,128)(2,1)} async-done(((bf16[3,128,1024]{2,1,0:T(8,128)(2,1)}), bf16[3,1024,1024]{2,1,0:T(8,128)(2,1)}) %all-gather.3.cloned.1.call-update) | async-done | bytes 6291472 | tf_op jit(solution)/shard_map/all_gather | solution.py:235
  179.2 4.6 %relax.1 = (f32[4,128,1024]{2,1,0:T(8,128)S(1)}, bf16[8,32,1024]{2,1,0:T(8,128)(2,1)S(1)}) custom-call(bf16[4,128,1024]{2,1,0:T(8,128)(2,1)S(1)} %copy-done.3, bf16[3,1024,1024]{2,1,0:T(8,128)(2,1)S(1)} %copy-done, bf16[1024,1024]{1,0:T(8,128)(2,1)S(1)} %copy-done.1, bf16[128,1024]{1,0:T(8,128)(2,1)S(1)} %broadcast_select_fusion.term_ref, ...), custom_call_target="tpu_custom_call" | custom-call | tf_op jit(solution)/shard_map/relax/pallas_call | solution.py:63
  186.0 5.1 %all-to-all-start = ((bf16[8,32,1024]{2,1,0:T(8,128)(2,1)}), bf16[8,32,1024]{2,1,0:T(8,128)(2,1)S(1)}, u32[]{:S(2)}, u32[]{:S(2)}) async-start(bf16[8,32,1024]{2,1,0:T(8,128)(2,1)} %copy-done.9), calls=%async_computation | async-start | bytes 1048576 | tf_op jit(solution)/shard_map/all_to_all | solution.py:244
  191.2 9.3 %all-to-all-done.pack_ref = bf16[8,32,1024]{2,1,0:T(8,128)(2,1)S(1)} async-done(((bf16[8,32,1024]{2,1,0:T(8,128)(2,1)}), bf16[8,32,1024]{2,1,0:T(8,128)(2,1)S(1)}, u32[]{:S(2)}, u32[]{:S(2)}) %all-to-all-start) | async-done | bytes 524320 | tf_op jit(solution)/shard_map/all_to_all | solution.py:244
  200.5 9.7 %chain.4 = (bf16[8,32,1024]{2,1,0:T(8,128)(2,1)}, bf16[16,1024]{1,0:T(8,128)(2,1)S(1)}) custom-call(s32[3]{0:T(128)S(1)} %pad_add_fusion.place_ref, bf16[8,32,1024]{2,1,0:T(8,128)(2,1)S(1)} %all-to-all-done.pack_ref, bf16[4,1024,1024]{2,1,0:T(8,128)(2,1)} %pad_maximum_fusion.own_ref, bf16[4,1024,1024]{2,1,0:T(8,128)(2,1)} %collective-permute-done.7.other_ref, ...), custom_call_target="tpu_custom_call" | custom-call | tf_op jit(solution)/shard_map/chain/pallas_call | solution.py:123
  211.4 3.4 collective-permute-done.8.in_ref
  214.8 9.7 %chain.5 = (bf16[8,32,1024]{2,1,0:T(8,128)(2,1)}, bf16[16,1024]{1,0:T(8,128)(2,1)S(1)}) custom-call(s32[3]{0:T(128)S(1)} %pad_add_fusion.place_ref, bf16[8,32,1024]{2,1,0:T(8,128)(2,1)S(1)} %all-to-all-done.pack_ref, bf16[4,1024,1024]{2,1,0:T(8,128)(2,1)} %pad_maximum_fusion.own_ref, bf16[4,1024,1024]{2,1,0:T(8,128)(2,1)} %collective-permute-done.7.other_ref, ...), custom_call_target="tpu_custom_call" | custom-call | tf_op jit(solution)/shard_map/chain/pallas_call | solution.py:123
  229.1 9.7 %chain.6 = (bf16[8,32,1024]{2,1,0:T(8,128)(2,1)}, bf16[16,1024]{1,0:T(8,128)(2,1)S(1)}) custom-call(s32[3]{0:T(128)S(1)} %pad_add_fusion.place_ref, bf16[8,32,1024]{2,1,0:T(8,128)(2,1)S(1)} %all-to-all-done.pack_ref, bf16[4,1024,1024]{2,1,0:T(8,128)(2,1)} %pad_maximum_fusion.own_ref, bf16[4,1024,1024]{2,1,0:T(8,128)(2,1)} %collective-permute-done.7.other_ref, ...), custom_call_target="tpu_custom_call" | custom-call | tf_op jit(solution)/shard_map/chain/pallas_call | solution.py:123
  243.6 9.6 %chain.7 = (bf16[8,32,1024]{2,1,0:T(8,128)(2,1)S(1)}, bf16[16,1024]{1,0:T(8,128)(2,1)}) custom-call(s32[3]{0:T(128)S(1)} %pad_add_fusion.place_ref, bf16[8,32,1024]{2,1,0:T(8,128)(2,1)S(1)} %all-to-all-done.pack_ref, bf16[4,1024,1024]{2,1,0:T(8,128)(2,1)} %pad_maximum_fusion.own_ref, bf16[4,1024,1024]{2,1,0:T(8,128)(2,1)} %collective-permute-done.7.other_ref, ...), custom_call_target="tpu_custom_call" | custom-call | tf_op jit(solution)/shard_map/chain/pallas_call | solution.py:123
  253.1 16.1 %all_to_all.10.spread_ref = bf16[8,32,1024]{2,1,0:T(8,128)(2,1)S(1)} all-to-all(bf16[8,32,1024]{2,1,0:T(8,128)(2,1)S(1)} %get-tuple-element.14), channel_id=1, replica_groups=mesh['zl'=4,'x'=4,'core'=2,'dp'=8,'mp'=2] {'x','core'}, dimensions={0} | all-to-all | bytes 1048576 | tf_op jit(solution)/shard_map/all_to_all | solution.py:252
  269.3 7.6 %correct.1 = (bf16[4,128,512]{2,1,0:T(8,128)(2,1)}, bf16[4,1024,512]{2,1,0:T(8,128)(2,1)S(1)}) custom-call(s32[3]{0:T(128)S(1)} %pad_add_fusion.place_ref, bf16[8,32,1024]{2,1,0:T(8,128)(2,1)S(1)} %all_to_all.10.spread_ref, bf16[4,128,1024]{2,1,0:T(8,128)(2,1)S(1)} %copy-done.3, f32[4,128,1024]{2,1,0:T(8,128)S(1)} %copy-done.5, ...), custom_call_target="tpu_custom_call" | custom-call | tf_op jit(solution)/shard_map/correct/pallas_call | solution.py:186
  278.9 55.3 %reduce-scatter.2.cloned.1.call-done = bf16[4,128,512]{2,1,0:T(8,128)(2,1)} async-done(((bf16[4,1024,512]{2,1,0:T(8,128)(2,1)}), bf16[4,128,512]{2,1,0:T(8,128)(2,1)}) %reduce-scatter.2.cloned.1.call-update) | async-done | bytes 524304 | tf_op jit(solution)/shard_map/reduce_scatter | solution.py:255
  (52 shorter events, 36.7 us)
Async XLA Ops:
  7.2 60.4 %all-gather.5.cloned.1.call-start = ((), (), s32[]{:S(2)}) async-start(), calls=%async_computation.4 | async-start | bytes 2359296 | tf_op jit(solution)/shard_map/all_gather | solution.py:234
  8.1 15.3 %collective-permute-start.1 = (bf16[128,512]{1,0:T(8,128)(2,1)S(1)}, bf16[128,512]{1,0:T(8,128)(2,1)S(1)}, u32[]{:S(2)}, u32[]{:S(2)}) collective-permute-start(bf16[128,512]{1,0:T(8,128)(2,1)S(1)} %slice_bitcast_fusion), channel_id=1, source_target_pairs={{0,1},{1,0},{2,3},{3,2},{4,5},{5,4},{6,7},{7,6},{8,9},{9,8},{10,11... | collective-permute-start | bytes 393224 | tf_op jit(solution)/shard_map/ppermute | solution.py:23
  24.3 151.2 %all-gather.3.cloned.1.call-start = ((), (), s32[]{:S(2)}) async-start(), calls=%async_computation.3 | async-start | bytes 7077888 | tf_op jit(solution)/shard_map/all_gather | solution.py:235
  67.6 45.7 %collective-permute-start.5 = (bf16[1024,1024]{1,0:T(8,128)(2,1)}, bf16[1024,1024]{1,0:T(8,128)(2,1)S(1)}, u32[]{:S(2)}, u32[]{:S(2)}) collective-permute-start(bf16[1024,1024]{1,0:T(8,128)(2,1)} %all-gather.5.cloned.1.call-done.coarse_ref), channel_id=1, source_target_pairs={{0,32},{32,64},{64,96},{96,0},{1,33},{33,65},{65,97},{97,1},{2,34}... | collective-permute-start | bytes 6291464 | tf_op jit(solution)/shard_map/ppermute | solution.py:28
  70.7 44.6 %collective-permute-start.3 = (bf16[1024,1024]{1,0:T(8,128)(2,1)}, bf16[1024,1024]{1,0:T(8,128)(2,1)}, u32[]{:S(2)}, u32[]{:S(2)}) collective-permute-start(bf16[1024,1024]{1,0:T(8,128)(2,1)} %all-gather.5.cloned.1.call-done.coarse_ref), channel_id=1, source_target_pairs={{0,96},{32,0},{64,32},{96,64},{1,97},{33,1},{65,33},{97,65},{2,98}... | collective-permute-start | bytes 6291464 | tf_op jit(solution)/shard_map/ppermute | solution.py:28
  75.1 14.9 %collective-permute-start = (bf16[3,128,512]{2,1,0:T(8,128)(2,1)S(1)}, bf16[3,128,512]{2,1,0:T(8,128)(2,1)S(1)}, u32[]{:S(2)}, u32[]{:S(2)}) collective-permute-start(bf16[3,128,512]{2,1,0:T(8,128)(2,1)S(1)} %slice.12), channel_id=1, source_target_pairs={{0,1},{1,0},{2,3},{3,2},{4,5},{5,4},{6,7},{7,6},{8,9},{9,8},{10,11... | collective-permute-start | bytes 1179656 | tf_op jit(solution)/shard_map/ppermute | solution.py:23
  113.2 2.1 copy-start.10
  113.3 22.2 %collective-permute-start.6 = (bf16[512,1024]{1,0:T(8,128)(2,1)S(1)}, bf16[512,1024]{1,0:T(8,128)(2,1)S(1)}, u32[]{:S(2)}, u32[]{:S(2)}) collective-permute-start(bf16[512,1024]{1,0:T(8,128)(2,1)S(1)} %slice.17), channel_id=1, source_target_pairs={{0,32},{32,64},{64,96},{96,0},{1,33},{33,65},{65,97},{97,1},{2,34}... | collective-permute-start | bytes 3145736 | tf_op jit(solution)/shard_map/ppermute | solution.py:28
  116.6 21.5 %copy-start.1 = (bf16[1024,1024]{1,0:T(8,128)(2,1)S(1)}, bf16[1024,1024]{1,0:T(8,128)(2,1)}, u32[]{:S(2)}) copy-start(bf16[1024,1024]{1,0:T(8,128)(2,1)} %all-gather.5.cloned.1.call-done.coarse_ref) | copy-start | bytes 6291460
  116.6 21.5 %copy-start.11 = (bf16[1024,1024]{1,0:T(8,128)(2,1)S(1)}, bf16[1024,1024]{1,0:T(8,128)(2,1)}, u32[]{:S(2)}) copy-start(bf16[1024,1024]{1,0:T(8,128)(2,1)} %copy-done.10) | copy-start | bytes 6291460
  116.6 21.3 %collective-permute-start.4 = (bf16[512,1024]{1,0:T(8,128)(2,1)S(1)}, bf16[512,1024]{1,0:T(8,128)(2,1)S(1)}, u32[]{:S(2)}, u32[]{:S(2)}) collective-permute-start(bf16[512,1024]{1,0:T(8,128)(2,1)S(1)} %slice.16), channel_id=1, source_target_pairs={{0,96},{32,0},{64,32},{96,64},{1,97},{33,1},{65,33},{97,65},{2,98}... | collective-permute-start | bytes 3145736 | tf_op jit(solution)/shard_map/ppermute | solution.py:28
  138.1 14.6 %copy-start.6 = (bf16[1,128,1024]{2,1,0:T(8,128)(2,1)S(1)}, bf16[1,128,1024]{2,1,0:T(8,128)(2,1)}, u32[]{:S(2)}) copy-start(bf16[1,128,1024]{2,1,0:T(8,128)(2,1)} %param.6) | copy-start | bytes 786436
  138.1 37.3 %copy-start.3 = (bf16[4,128,1024]{2,1,0:T(8,128)(2,1)S(1)}, bf16[4,128,1024]{2,1,0:T(8,128)(2,1)}, u32[]{:S(2)}) copy-start(bf16[4,128,1024]{2,1,0:T(8,128)(2,1)} %states_ref.3) | copy-start | bytes 3145732
  144.0 56.5 %collective-permute-start.7 = (bf16[4,1024,1024]{2,1,0:T(8,128)(2,1)}, bf16[4,1024,1024]{2,1,0:T(8,128)(2,1)}, u32[]{:S(2)}, u32[]{:S(2)}) collective-permute-start(bf16[4,1024,1024]{2,1,0:T(8,128)(2,1)} %pad_maximum_fusion.own_ref), channel_id=1, source_target_pairs={{0,16},{16,0},{1,17},{17,1},{2,18},{18,2},{3,19},{19,3},{4,20},{20... | collective-permute-start | bytes 25165832 | tf_op jit(solution)/shard_map/ppermute | solution.py:23
  152.8 13.5 %collective-permute-start.2 = (bf16[128,1024]{1,0:T(8,128)(2,1)S(1)}, bf16[128,1024]{1,0:T(8,128)(2,1)}, u32[]{:S(2)}, u32[]{:S(2)}) collective-permute-start(bf16[128,1024]{1,0:T(8,128)(2,1)S(1)} %bitcast.12), channel_id=1, source_target_pairs={{16,0},{32,16},{48,32},{64,48},{80,64},{96,80},{112,96},{128,112},... | collective-permute-start | bytes 786440 | tf_op jit(solution)/shard_map/ppermute | solution.py:232
  175.5 2.8 copy-start
  186.0 14.4 %all-to-all-start = ((bf16[8,32,1024]{2,1,0:T(8,128)(2,1)}), bf16[8,32,1024]{2,1,0:T(8,128)(2,1)S(1)}, u32[]{:S(2)}, u32[]{:S(2)}) async-start(bf16[8,32,1024]{2,1,0:T(8,128)(2,1)} %copy-done.9), calls=%async_computation | async-start | bytes 1048576 | tf_op jit(solution)/shard_map/all_to_all | solution.py:244
  191.1 143.1 %reduce-scatter.2.cloned.1.call-start = ((), (), s32[]{:S(2)}) async-start(), calls=%async_computation.5 | async-start | bytes 4718592 | tf_op jit(solution)/shard_map/reduce_scatter | solution.py:255
  210.2 4.6 %collective-permute-start.8 = (bf16[16,1024]{1,0:T(8,128)(2,1)S(1)}, bf16[16,1024]{1,0:T(8,128)(2,1)S(1)}, u32[]{:S(2)}, u32[]{:S(2)}) collective-permute-start(bf16[16,1024]{1,0:T(8,128)(2,1)S(1)} %get-tuple-element.11), channel_id=1, source_target_pairs={{128,0},{256,128},{384,256},{129,1},{257,129},{385,257},{130,2},{2... | collective-permute-start | bytes 98312 | tf_op jit(solution)/shard_map/ppermute | solution.py:251
  224.5 4.6 %collective-permute-start.9 = (bf16[16,1024]{1,0:T(8,128)(2,1)S(1)}, bf16[16,1024]{1,0:T(8,128)(2,1)S(1)}, u32[]{:S(2)}, u32[]{:S(2)}) collective-permute-start(bf16[16,1024]{1,0:T(8,128)(2,1)S(1)} %get-tuple-element.12), channel_id=1, source_target_pairs={{128,0},{256,128},{384,256},{129,1},{257,129},{385,257},{130,2},{2... | collective-permute-start | bytes 98312 | tf_op jit(solution)/shard_map/ppermute | solution.py:251
  238.8 30.5 %copy-start.8 = (bf16[1,128,1024]{2,1,0:T(8,128)(2,1)S(1)}, bf16[1,128,1024]{2,1,0:T(8,128)(2,1)}, u32[]{:S(2)}) copy-start(bf16[1,128,1024]{2,1,0:T(8,128)(2,1)} %param.6) | copy-start | bytes 786436
  238.8 4.8 %collective-permute-start.10 = (bf16[16,1024]{1,0:T(8,128)(2,1)S(1)}, bf16[16,1024]{1,0:T(8,128)(2,1)S(1)}, u32[]{:S(2)}, u32[]{:S(2)}) collective-permute-start(bf16[16,1024]{1,0:T(8,128)(2,1)S(1)} %get-tuple-element.13), channel_id=1, source_target_pairs={{128,0},{256,128},{384,256},{129,1},{257,129},{385,257},{130,2},{2... | collective-permute-start | bytes 98312 | tf_op jit(solution)/shard_map/ppermute | solution.py:251
  243.6 25.7 %copy-start.5 = (f32[4,128,1024]{2,1,0:T(8,128)S(1)}, f32[4,128,1024]{2,1,0:T(8,128)}, u32[]{:S(2)}) copy-start(f32[4,128,1024]{2,1,0:T(8,128)} %copy-done.4) | copy-start | bytes 6291460
  276.9 2.0 copy-start.2
  (3 other events, 3.1 us)
Sparse Core Ops, SparseCore 0:
  24.4 43.1 all-gather.4
  91.2 84.1 all-gather.2
  279.0 55.1 reduce-scatter.1

commit v2 on v1

v2 whole, which is shorter than its diff:
```python
import functools

import jax
import jax.numpy as jnp
from jax import lax
from jax.experimental import pallas as pl
from jax.experimental.pallas import tpu as pltpu
from jax.sharding import Mesh
from jax.sharding import PartitionSpec as P

step_size = 0.1
BF = jnp.bfloat16
F32 = jnp.float32
LAYER = ("zl", "x", "core")
RING = ("x", "core")


def back_product(scaled, weight):
    return lax.dot_general(scaled, weight, (((1,), (1,)), ((), ())), preferred_element_type=F32)


def swapped(value, axis):
    return lax.ppermute(value, axis, [(0, 1), (1, 0)])


def rotated(value, axis, steps):
    count = lax.axis_size(axis)
    return lax.ppermute(value, axis, [(i, (i + steps) % count) for i in range(count)])


def halves(value, index):
    half = value.shape[1] // 2
    low, high = value[:, :half], value[:, half:]
    return jnp.where(index == 0, low, high), jnp.where(index == 0, high, low)


def params(mib):
    return pltpu.CompilerParams(vmem_limit_bytes=mib * 2**20)


def cost(flops, moved):
    return pl.CostEstimate(flops=flops, bytes_accessed=moved, transcendentals=0)


def slope_kernel(states_ref, weight_ref, out_ref):
    tangent = jnp.tanh(jnp.dot(states_ref[0], weight_ref[0], preferred_element_type=F32))
    out_ref[0] = 1.0 - tangent * tangent


def slopes_of(states, weights, first):
    rows, width = states.shape[1:]
    layers, _, columns = weights.shape
    return pl.pallas_call(
        slope_kernel,
        grid=(layers,),
        in_specs=[
            pl.BlockSpec((1, rows, width), lambda t: (first + t, 0, 0)),
            pl.BlockSpec((1, width, columns), lambda t: (t, 0, 0)),
        ],
        out_specs=pl.BlockSpec((1, rows, columns), lambda t: (t, 0, 0)),
        out_shape=jax.ShapeDtypeStruct((layers, rows, columns), F32),
        compiler_params=params(56),
        cost_estimate=cost(2 * layers * rows * width * columns, 2 * layers * width * columns),
        name="slopes",
    )(states, weights)


def first_kernel(place_ref, term_ref, states_ref, weight_ref, keep_ref, send_ref):
    weight = weight_ref[0]
    tangent = jnp.tanh(jnp.dot(states_ref[0], weight, preferred_element_type=F32))
    upper = halves(term_ref[...], place_ref[2])[0].astype(F32)
    scaled = (upper * (1.0 - tangent * tangent)).astype(BF)
    own, other = halves(step_size * back_product(scaled, weight), place_ref[2])
    keep_ref[...] = upper + own
    send_ref[...] = other.astype(BF)


def middle_kernel(full, place_ref, kept_ref, got_ref, slope_ref, weight_ref, keep_ref, send_ref):
    upper = kept_ref[...] + got_ref[...].astype(F32)
    scaled = (upper * slope_ref[0]).astype(BF)
    product = step_size * back_product(scaled, weight_ref[0])
    if full:
        none = jnp.zeros_like(upper)
        first = place_ref[2] == 0
        sides = [jnp.where(first, upper, none), jnp.where(first, none, upper)]
        mine = product + jnp.concatenate(sides, 1)
        keep_ref[...] = mine
        send_ref[...] = mine.astype(BF)
    else:
        own, other = halves(product, place_ref[2])
        keep_ref[...] = upper + own
        send_ref[...] = other.astype(BF)


def half_step(place, operands, states, slopes, weights, layer, full=False):
    rows, width = states.shape[1:]
    columns = width if full else width // 2
    flat = [pl.BlockSpec(v.shape, lambda t, place: (0, 0)) for v in operands]
    pick = lambda v, i: pl.BlockSpec((1,) + v.shape[1:], lambda t, place: (i, 0, 0))
    if slopes is None:
        kernel, source, index = first_kernel, states, layer
    else:
        kernel, source, index = functools.partial(middle_kernel, full), slopes, layer - 1
    return pl.pallas_call(
        kernel,
        grid_spec=pltpu.PrefetchScalarGridSpec(
            num_scalar_prefetch=1,
            grid=(1,),
            in_specs=flat + [pick(source, index), pick(weights, layer - 1)],
            out_specs=[pl.BlockSpec((rows, columns), lambda t, place: (0, 0))] * 2,
        ),
        out_shape=[
            jax.ShapeDtypeStruct((rows, columns), F32),
            jax.ShapeDtypeStruct((rows, columns), BF),
        ],
        compiler_params=params(56 if slopes is None else 12),
        cost_estimate=cost(rows * width * width, width * width),
        name="half_step",
    )(place, *operands, source, weights)


def last_kernel(blocks, kept_ref, got_ref, slope_ref, weight_ref, guess_ref, pack_ref):
    rows, width = kept_ref.shape
    part = rows // blocks
    upper = kept_ref[...] + got_ref[...].astype(F32)
    slope = slope_ref[0]
    scaled = (upper * slope).astype(BF)
    relaxed = upper + step_size * back_product(scaled, weight_ref[...])
    residual = relaxed - guess_ref[...].astype(F32)
    pack_ref[:, :part, :] = residual.astype(BF).reshape(blocks, part, width)
    pack_ref[:, part:, :] = slope.astype(BF).reshape(blocks, part, width)


def last_step(kept, got, slope, weight, guess, blocks):
    rows, width = kept.shape
    return pl.pallas_call(
        functools.partial(last_kernel, blocks),
        out_shape=jax.ShapeDtypeStruct((blocks, 2 * rows // blocks, width), BF),
        compiler_params=params(16),
        cost_estimate=cost(2 * rows * width * width, 2 * width * width),
        name="last_step",
    )(kept, got, slope, weight, guess)


def chain_kernel(place_ref, pack_ref, in_ref, *rest):
    chips = (len(rest) - 4) // 2
    sources, (out_ref, low_ref, held, arrived) = rest[: 2 * chips], rest[2 * chips :]
    count = 2 * chips
    part = in_ref.shape[0]
    scale = 4 * step_size

    def fetch(source, point):
        return pltpu.make_async_copy(source, held.at[point], arrived.at[point])

    for point in range(count - 1, -1, -1):
        hop = lax.rem(point // 2 - place_ref[0] + chips, chips)
        same = place_ref[1] == point % 2
        for number in range(chips):
            @pl.when((hop == number) & same)
            def _():
                fetch(sources[number], point).start()

            @pl.when((hop == number) & jnp.logical_not(same))
            def _():
                fetch(sources[chips + number], point).start()

    short = in_ref[...]
    for point in range(count - 1, -1, -1):
        v = short.astype(F32)
        scaled = (v * pack_ref[point, part:, :].astype(F32)).astype(BF)
        out_ref[point, :part, :] = short
        residual = pack_ref[point, :part, :].astype(F32)
        fetch(sources[0], point).wait()
        short = (v + scale * back_product(scaled, held[point]) + residual).astype(BF)
        out_ref[point, part:, :] = short
    low_ref[...] = short


def chain(place, pack, sources, incoming):
    count = len(sources)
    weight = sources[0].shape
    whole = lambda v: pl.BlockSpec(v.shape, lambda t, place: (0,) * v.ndim)
    return pl.pallas_call(
        chain_kernel,
        grid_spec=pltpu.PrefetchScalarGridSpec(
            num_scalar_prefetch=1,
            grid=(1,),
            in_specs=[whole(pack), whole(incoming)] + [pl.BlockSpec(memory_space=pl.ANY)] * count,
            out_specs=[whole(pack), whole(incoming)],
            scratch_shapes=[
                pltpu.VMEM((count,) + weight, BF),
                pltpu.SemaphoreType.DMA((count,)),
            ],
        ),
        out_shape=[
            jax.ShapeDtypeStruct(pack.shape, BF),
            jax.ShapeDtypeStruct(incoming.shape, BF),
        ],
        compiler_params=params(40),
        cost_estimate=cost(2 * pack.size * weight[0], 2 * count * weight[0] * weight[1]),
        name="chain",
    )(place, pack, incoming, *sources)


def correct_kernel(
    place_ref, spread_ref, states_ref, slope_a, slope_b, weight_a, weight_b, slope_ref,
    term_ref, guess_ref, adj_ref, part_ref, own_ref, other_ref,
):
    turn = pl.program_id(0)
    last = pl.num_programs(0) - 1
    rows, width = term_ref.shape
    part = spread_ref.shape[1] // 2

    def split(value):
        return halves(value, place_ref[2])

    def terms(scaled):
        product = lax.dot_general(
            states_ref[0], scaled, (((0,), (0,)), ((), ())), preferred_element_type=F32
        )
        part_ref[0] = product.astype(BF)

    @pl.when(turn == 0)
    def _():
        error = spread_ref[:, :part, :].reshape(rows, width).astype(F32)
        own_ref[...], other_ref[...] = split(term_ref[...].astype(F32) + error)

    @pl.when(turn < last)
    def _():
        scaled = (own_ref[...] * slope_a[0]).astype(BF)
        scaled_other = (other_ref[...] * slope_b[0]).astype(BF)
        terms(scaled)
        product = back_product(scaled, weight_a[0]) + back_product(scaled_other, weight_b[0])
        own, other = split(step_size * product)
        current = own_ref[...] + own
        own_ref[...] = current
        other_ref[...] += other
        adj_ref[0] = current.astype(BF)

    @pl.when(turn == last)
    def _():
        terms((own_ref[...] * split(slope_ref[0])[0]).astype(BF))
        error = spread_ref[:, part:, :].reshape(rows, width).astype(F32)
        adj_ref[0] = split(guess_ref[...].astype(F32) + error)[0].astype(BF)


def correct(place, spread, states, slopes_a, slopes_b, weights_a, weights_b, slope, terminal, guess):
    layers, rows, width = states.shape
    half = width // 2
    top = layers - 1
    lower = lambda t, place: (jnp.maximum(top - 1 - t, 0), 0, 0)
    whole = lambda v: pl.BlockSpec(v.shape, lambda t, place: (0,) * v.ndim)
    layer = lambda v: pl.BlockSpec((1,) + v.shape[1:], lower)
    return pl.pallas_call(
        correct_kernel,
        grid_spec=pltpu.PrefetchScalarGridSpec(
            num_scalar_prefetch=1,
            grid=(layers,),
            in_specs=[
                whole(spread),
                pl.BlockSpec((1, rows, width), lambda t, place: (top - t, 0, 0)),
                layer(slopes_a),
                layer(slopes_b),
                layer(weights_a),
                layer(weights_b),
                whole(slope),
                whole(terminal),
                whole(guess),
            ],
            out_specs=[
                pl.BlockSpec((1, rows, half), lambda t, place: (top - t, 0, 0)),
                pl.BlockSpec((1, width, half), lambda t, place: (top - t, 0, 0)),
            ],
            scratch_shapes=[pltpu.VMEM((rows, half), F32)] * 2,
        ),
        out_shape=[
            jax.ShapeDtypeStruct((layers, rows, half), BF),
            jax.ShapeDtypeStruct((layers, width, half), BF),
        ],
        compiler_params=params(56),
        name="correct",
    )(place, spread, states, slopes_a, slopes_b, weights_a, weights_b, slope, terminal, guess)


def put(buffer, value, *index):
    lead = len(index)
    start = tuple(index) + (0,) * (buffer.ndim - lead)
    return lax.dynamic_update_slice(buffer, value.reshape((1,) * lead + value.shape), start)


def ring_gather(piece, beside):
    count = lax.axis_size("dp")
    me = lax.axis_index("dp")
    rows = piece.shape[0]
    mid = rows // 2
    whole = put(jnp.zeros((count,) + piece.shape, piece.dtype), piece, me)
    up = down = piece
    for hop in range(1, count // 2):
        if hop == count // 2 - 1:
            up, down, beside = lax.optimization_barrier((up, down, beside))
        up, down = rotated(up, "dp", 1), rotated(down, "dp", -1)
        whole = put(whole, up, (me - hop) % count)
        whole = put(whole, down, (me + hop) % count)
    far = jnp.concatenate([rotated(up[:mid], "dp", 1), rotated(down[mid:], "dp", -1)], 0)
    whole = put(whole, far, (me + count // 2) % count)
    return whole.reshape((count * rows,) + piece.shape[1:]), beside


def body(states, weights, guess_points, cotangent):
    slabs = lax.axis_size(LAYER)
    slab = lax.axis_index(LAYER)
    half_index = lax.axis_index("mp")
    place = jnp.stack([lax.axis_index("x"), lax.axis_index("core"), half_index]).astype(jnp.int32)
    blocks = lax.axis_size(RING)
    layers, rows, width = states.shape
    mid = width // 2
    guess = guess_points[0]

    rest_own = lax.all_gather(weights[1:], "dp", axis=1, tiled=True)
    shard, far_shard = weights[0], swapped(weights[0], "mp")
    shard = jnp.where(
        half_index == 0,
        jnp.concatenate([shard, far_shard], -1),
        jnp.concatenate([far_shard, shard], -1),
    )
    coarse, rest_far = ring_gather(shard, swapped(weights[1:], "mp"))
    rest_other = lax.all_gather(rest_far, "dp", axis=1, tiled=True)
    next_guess = lax.ppermute(guess, LAYER, [(i, i - 1) for i in range(1, slabs)])
    terminal = jnp.where(slab == slabs - 1, cotangent, next_guess)
    slope = slopes_of(states, coarse[None], 0)

    ahead = rotated(coarse, "x", -1)
    behind = rotated(coarse, "x", 1)
    slopes_own = slopes_of(states, rest_own, 1)
    keep, send = half_step(place, (terminal,), states, None, rest_own, layers - 1)
    got = swapped(send, "mp")
    for layer in range(layers - 2, 0, -1):
        keep, send = half_step(place, (keep, got), states, slopes_own, rest_own, layer, layer == 1)
        got = swapped(send, "mp")
    pack = last_step(keep, got, slope, coarse, guess, blocks)
    ahead, behind, pack = lax.optimization_barrier((ahead, behind, pack))
    front, back = rotated(ahead[:mid], "x", -1), rotated(behind[mid:], "x", 1)
    pack = lax.all_to_all(pack, RING, 0, 0, tiled=True)
    front, back, pack = lax.optimization_barrier((front, back, pack))
    across = jnp.concatenate([front, back], 0)
    ring = (coarse, ahead, across, behind)
    ring = ring + tuple(swapped(value, "core") for value in ring)
    slopes_other = slopes_of(states, rest_other, 1)

    incoming = jnp.zeros((pack.shape[1] // 2, width), BF)
    stages = lax.axis_size("zl")
    for stage in range(stages):
        errors, lowest = chain(place, pack, ring, incoming)
        if stage < stages - 1:
            incoming = lax.ppermute(lowest, "zl", [(i, i - 1) for i in range(1, stages)])
    spread = lax.all_to_all(errors, RING, 0, 0, tiled=True)

    adjoint, partial = correct(
        place, spread, states, slopes_own, slopes_other, rest_own, rest_other, slope, terminal, guess
    )
    grads = lax.psum_scatter(partial, "dp", scatter_dimension=1, tiled=True)
    return adjoint, step_size * grads.astype(F32)


def solution(mesh):
    slabs, rows, halves = (mesh.shape[name] for name in ("layer", "dp", "mp"))
    fine = Mesh(
        mesh.devices.reshape(slabs // 8, 4, 2, rows, halves), ("zl", "x", "core", "dp", "mp")
    )
    return jax.shard_map(
        body,
        mesh=fine,
        in_specs=(
            P(LAYER, "dp", None),
            P(LAYER, "dp", "mp"),
            P(LAYER, "dp", None),
            P("dp", None),
        ),
        out_specs=(P(LAYER, "dp", "mp"), P(LAYER, "dp", "mp")),
        check_vma=False,
    )
```

time: 344 us -> 384 us (1.12)
  starting transfers between devices: 52.2 us -> 107 us
  blocking collectives: 16.1 us -> 0 us
  waiting for transfers between devices: 187 us -> 172 us
  Pallas kernels: 50.8 us -> 63.4 us
  local copies, waits for them, and re-layouts: 11.2 us -> 20 us
  other arithmetic: 11.1 us -> 5.07 us
    all_gather x2, waiting for transfers between devices: 51.5 us -> 0.01 us  [the longest x1 0.01 us: body(): rest_own = lax.all_gather(weights[1:], 'dp', axis=1, tiled=True)]
    ppermute x1, waiting for transfers between devices: 11.5 us -> 40.2 us  [body(): lax.ppermute(guess, LAYER, [(i, i - 1) for i in range(1, slabs)])]
    ppermute x4 -> x12, starting transfers between devices: 13.2 us -> 38.4 us  [rotated(): lax.ppermute(value, axis, [(i, (i + steps) % count) for i in range(count)])]
    ppermute x4 -> x12, waiting for transfers between devices: 38.6 us -> 16.9 us  [rotated(): lax.ppermute(value, axis, [(i, (i + steps) % count) for i in range(count)])]
    ppermute x3 -> x9, starting transfers between devices: 27.9 us -> 44.5 us  [swapped(): return lax.ppermute(value, axis, [(0, 1), (1, 0)])]
    all_to_all x1 -> x0, blocking collectives: 16.1 us -> none  [body(): spread = lax.all_to_all(errors, RING, 0, 0, tiled=True)]
    pallas_call x5 -> x11, Pallas kernels: 43.2 us -> 53.6 us  [the longest x4 33.5 us: chain(): pl.pallas_call(chain_kernel, grid_spec=pltpu.PrefetchScalarGridSpec(num_s...]
    all_to_all x1, waiting for transfers between devices: 9.27 us -> 19.5 us  [body(): pack = lax.all_to_all(pack, RING, 0, 0, tiled=True)]
  transfers between devices with their start and end apart: 15 -> 30, of which waited for: 13 -> 16; matrix products, arithmetic and copies ran while one was open for 3% -> 4% of each run, Pallas kernels for 1% -> 14%
where the time goes in v2:
time: 384 us; the launch traced here: 382 us
  waiting for transfers between devices  172 us (45%)
  starting transfers between devices  107 us (28%)
  Pallas kernels  63.4 us (17%)
  local copies, waits for them, and re-layouts  20 us (5%)
  between operations  14.3 us (4%)
  other arithmetic  5.07 us (1%)
    reduce_scatter x1, waiting for transfers between devices, body(): grads = lax.psum_scatter(partial, 'dp', scatter_dimension=1, tiled=True)  56.3 us
    ppermute x9, starting transfers between devices, swapped(): return lax.ppermute(value, axis, [(0, 1), (1, 0)])  44.5 us
    ppermute x1, waiting for transfers between devices, body(): lax.ppermute(guess, LAYER, [(i, i - 1) for i in range(1, slabs)])  40.2 us
    ppermute x12, starting transfers between devices, rotated(): lax.ppermute(value, axis, [(i, (i + steps) % count) for i in range(count)])  38.4 us
    pallas_call x4, Pallas kernels, chain(): pl.pallas_call(chain_kernel, grid_spec=pltpu.PrefetchScalarGridSpec(num_s...  33.5 us
    all_to_all x1, waiting for transfers between devices, body(): pack = lax.all_to_all(pack, RING, 0, 0, tiled=True)  19.5 us
    ppermute x3, waiting for transfers between devices, body(): lax.ppermute(lowest, 'zl', [(i, i - 1) for i in range(1, stages)])  18.2 us
    ppermute x12, waiting for transfers between devices, rotated(): lax.ppermute(value, axis, [(i, (i + steps) % count) for i in range(count)])  16.9 us
  transfers between devices with their start and end apart: 30, of which 16 were waited for; matrix products, arithmetic and copies ran while one was open for 4% of the time, Pallas kernels for 14%

profile of v2, /device:TPU:1, one launch (start us, length us, event | category | flops | bytes accessed | tf_op | source)
XLA Modules:
  0.0 382.0 jit_solution(15256773773219957637)
XLA Ops:
  10.0 11.5 %collective-permute-start = (bf16[128,512]{1,0:T(8,128)(2,1)S(1)}, bf16[128,512]{1,0:T(8,128)(2,1)S(1)}, u32[]{:S(2)}, u32[]{:S(2)}) collective-permute-start(bf16[128,512]{1,0:T(8,128)(2,1)S(1)} %get-tuple-element.45), channel_id=1, source_target_pairs={{0,1},{1,0},{2,3},{3,2},{4,5},{5,4},{6,7},{7,6},{8,9},{9,8},{10,11... | collective-permute-start | bytes 393224 | tf_op jit(solution)/shard_map/ppermute | solution.py:23
  31.9 8.2 %collective-permute-start.5 = (bf16[3,128,512]{2,1,0:T(8,128)(2,1)}, bf16[3,128,512]{2,1,0:T(8,128)(2,1)S(1)}, u32[]{:S(2)}, u32[]{:S(2)}) collective-permute-start(bf16[3,128,512]{2,1,0:T(8,128)(2,1)} %slice.21), channel_id=1, source_target_pairs={{0,1},{1,0},{2,3},{3,2},{4,5},{5,4},{6,7},{7,6},{8,9},{9,8},{10,11... | collective-permute-start | bytes 1179656 | tf_op jit(solution)/shard_map/ppermute | solution.py:23
  44.5 4.6 %collective-permute-start.4 = (bf16[128,1024]{1,0:T(8,128)(2,1)S(1)}, bf16[128,1024]{1,0:T(8,128)(2,1)S(1)}, u32[]{:S(2)}, u32[]{:S(2)}) collective-permute-start(bf16[128,1024]{1,0:T(8,128)(2,1)S(1)} %collective-permute-done.2), channel_id=1, source_target_pairs={{0,14},{2,0},{4,2},{6,4},{8,6},{10,8},{12,10},{14,12},{1,15},{3,1}... | collective-permute-start | bytes 786440 | tf_op jit(solution)/shard_map/ppermute | solution.py:28
  50.6 8.0 %collective-permute-done.3 = bf16[128,1024]{1,0:T(8,128)(2,1)S(1)} collective-permute-done((bf16[128,1024]{1,0:T(8,128)(2,1)S(1)}, bf16[128,1024]{1,0:T(8,128)(2,1)S(1)}, u32[]{:S(2)}, u32[]{:S(2)}) %collective-permute-start.3) | collective-permute-done | bytes 262176 | tf_op jit(solution)/shard_map/ppermute | solution.py:28
  61.9 4.8 %collective-permute-start.7 = (bf16[128,1024]{1,0:T(8,128)(2,1)S(1)}, bf16[128,1024]{1,0:T(8,128)(2,1)S(1)}, u32[]{:S(2)}, u32[]{:S(2)}) collective-permute-start(bf16[128,1024]{1,0:T(8,128)(2,1)S(1)} %collective-permute-done.4), channel_id=1, source_target_pairs={{0,14},{2,0},{4,2},{6,4},{8,6},{10,8},{12,10},{14,12},{1,15},{3,1}... | collective-permute-start | bytes 786440 | tf_op jit(solution)/shard_map/ppermute | solution.py:28
  68.1 7.6 %collective-permute-done.6 = bf16[128,1024]{1,0:T(8,128)(2,1)S(1)} collective-permute-done((bf16[128,1024]{1,0:T(8,128)(2,1)S(1)}, bf16[128,1024]{1,0:T(8,128)(2,1)S(1)}, u32[]{:S(2)}, u32[]{:S(2)}) %collective-permute-start.6) | collective-permute-done | bytes 262176 | tf_op jit(solution)/shard_map/ppermute | solution.py:28
  90.2 6.5 %collective-permute-start.12 = (bf16[128,1024]{1,0:T(8,128)(2,1)S(1)}, bf16[128,1024]{1,0:T(8,128)(2,1)S(1)}, u32[]{:S(2)}, u32[]{:S(2)}) collective-permute-start(bf16[128,1024]{1,0:T(8,128)(2,1)S(1)} %bitcast.26), channel_id=1, source_target_pairs={{16,0},{32,16},{48,32},{64,48},{80,64},{96,80},{112,96},{128,112},... | collective-permute-start | bytes 786440 | tf_op jit(solution)/shard_map/ppermute | solution.py:328
  97.3 40.2 %collective-permute-done.12 = bf16[128,1024]{1,0:T(8,128)(2,1)S(1)} collective-permute-done((bf16[128,1024]{1,0:T(8,128)(2,1)S(1)}, bf16[128,1024]{1,0:T(8,128)(2,1)S(1)}, u32[]{:S(2)}, u32[]{:S(2)}) %collective-permute-start.12) | collective-permute-done | bytes 262176 | tf_op jit(solution)/shard_map/ppermute | solution.py:328
  141.8 5.3 %collective-permute-start.13 = (bf16[128,512]{1,0:T(8,128)(2,1)}, bf16[128,512]{1,0:T(8,128)(2,1)S(1)}, u32[]{:S(2)}, u32[]{:S(2)}) collective-permute-start(bf16[128,512]{1,0:T(8,128)(2,1)} %get-tuple-element.26), channel_id=1, source_target_pairs={{0,1},{1,0},{2,3},{3,2},{4,5},{5,4},{6,7},{7,6},{8,9},{9,8},{10,11... | collective-permute-start | bytes 393224 | tf_op jit(solution)/shard_map/ppermute | solution.py:23
  154.1 5.0 %collective-permute-start.14 = (bf16[128,512]{1,0:T(8,128)(2,1)S(1)}, bf16[128,512]{1,0:T(8,128)(2,1)S(1)}, u32[]{:S(2)}, u32[]{:S(2)}) collective-permute-start(bf16[128,512]{1,0:T(8,128)(2,1)S(1)} %get-tuple-element.28), channel_id=1, source_target_pairs={{0,1},{1,0},{2,3},{3,2},{4,5},{5,4},{6,7},{7,6},{8,9},{9,8},{10,11... | collective-permute-start | bytes 393224 | tf_op jit(solution)/shard_map/ppermute | solution.py:23
  164.8 5.0 %collective-permute-start.15 = (bf16[128,1024]{1,0:T(8,128)(2,1)S(1)}, bf16[128,1024]{1,0:T(8,128)(2,1)S(1)}, u32[]{:S(2)}, u32[]{:S(2)}) collective-permute-start(bf16[128,1024]{1,0:T(8,128)(2,1)S(1)} %get-tuple-element.30), channel_id=1, source_target_pairs={{0,1},{1,0},{2,3},{3,2},{4,5},{5,4},{6,7},{7,6},{8,9},{9,8},{10,11... | collective-permute-start | bytes 786440 | tf_op jit(solution)/shard_map/ppermute | solution.py:23
  190.9 7.4 %all-to-all-start = ((bf16[8,32,1024]{2,1,0:T(8,128)(2,1)}), bf16[8,32,1024]{2,1,0:T(8,128)(2,1)S(1)}, u32[]{:S(2)}, u32[]{:S(2)}) async-start(bf16[8,32,1024]{2,1,0:T(8,128)(2,1)} %last_step.1), calls=%async_computation | async-start | bytes 1048576 | tf_op jit(solution)/shard_map/all_to_all | solution.py:343
  204.6 19.5 %all-to-all-done.pack_ref = bf16[8,32,1024]{2,1,0:T(8,128)(2,1)S(1)} async-done(((bf16[8,32,1024]{2,1,0:T(8,128)(2,1)}), bf16[8,32,1024]{2,1,0:T(8,128)(2,1)S(1)}, u32[]{:S(2)}, u32[]{:S(2)}) %all-to-all-start) | async-done | bytes 524320 | tf_op jit(solution)/shard_map/all_to_all | solution.py:343
  235.1 8.4 %chain.4 = (bf16[8,32,1024]{2,1,0:T(8,128)(2,1)}, bf16[16,1024]{1,0:T(8,128)(2,1)S(1)}) custom-call(s32[3]{0:T(128)S(1)} %copy-done.6, bf16[8,32,1024]{2,1,0:T(8,128)(2,1)S(1)} %all-to-all-done.pack_ref, bf16[16,1024]{1,0:T(8,128)(2,1)S(1)} %broadcast_in_dim.7.in_ref, bf16[1024,1024]{1,0:T(8,128)(2,1)} %bitcast.12.weight_ref.rest_0_, ...), custom_call_target="tpu_custom_call" | custom-call | flops 536870912 | bytes 16777216 | tf_op jit(solution)/shard_map/chain/pallas_call | solution.py:183
  244.8 5.8 %collective-permute-done.22.in_ref = bf16[16,1024]{1,0:T(8,128)(2,1)S(1)} collective-permute-done((bf16[16,1024]{1,0:T(8,128)(2,1)S(1)}, bf16[16,1024]{1,0:T(8,128)(2,1)S(1)}, u32[]{:S(2)}, u32[]{:S(2)}) %collective-permute-start.22) | collective-permute-done | bytes 32800 | tf_op jit(solution)/shard_map/ppermute | solution.py:355
  250.5 8.4 %chain.5 = (bf16[8,32,1024]{2,1,0:T(8,128)(2,1)}, bf16[16,1024]{1,0:T(8,128)(2,1)S(1)}) custom-call(s32[3]{0:T(128)S(1)} %copy-done.6, bf16[8,32,1024]{2,1,0:T(8,128)(2,1)S(1)} %all-to-all-done.pack_ref, bf16[16,1024]{1,0:T(8,128)(2,1)S(1)} %collective-permute-done.22.in_ref, bf16[1024,1024]{1,0:T(8,128)(2,1)} %bitcast.12.weight_ref.rest_0_, ...), custom_call_target="tpu_custom_call" | custom-call | flops 536870912 | bytes 16777216 | tf_op jit(solution)/shard_map/chain/pallas_call | solution.py:183
  260.2 5.9 %collective-permute-done.23.in_ref = bf16[16,1024]{1,0:T(8,128)(2,1)S(1)} collective-permute-done((bf16[16,1024]{1,0:T(8,128)(2,1)S(1)}, bf16[16,1024]{1,0:T(8,128)(2,1)S(1)}, u32[]{:S(2)}, u32[]{:S(2)}) %collective-permute-start.23) | collective-permute-done | bytes 32800 | tf_op jit(solution)/shard_map/ppermute | solution.py:355
  266.1 8.4 %chain.6 = (bf16[8,32,1024]{2,1,0:T(8,128)(2,1)}, bf16[16,1024]{1,0:T(8,128)(2,1)S(1)}) custom-call(s32[3]{0:T(128)S(1)} %copy-done.6, bf16[8,32,1024]{2,1,0:T(8,128)(2,1)S(1)} %all-to-all-done.pack_ref, bf16[16,1024]{1,0:T(8,128)(2,1)S(1)} %collective-permute-done.23.in_ref, bf16[1024,1024]{1,0:T(8,128)(2,1)} %bitcast.12.weight_ref.rest_0_, ...), custom_call_target="tpu_custom_call" | custom-call | flops 536870912 | bytes 16777216 | tf_op jit(solution)/shard_map/chain/pallas_call | solution.py:183
  275.7 6.5 %collective-permute-done.24.in_ref = bf16[16,1024]{1,0:T(8,128)(2,1)S(1)} collective-permute-done((bf16[16,1024]{1,0:T(8,128)(2,1)S(1)}, bf16[16,1024]{1,0:T(8,128)(2,1)S(1)}, u32[]{:S(2)}, u32[]{:S(2)}) %collective-permute-start.24) | collective-permute-done | bytes 32800 | tf_op jit(solution)/shard_map/ppermute | solution.py:355
  282.3 8.4 %chain.7 = (bf16[8,32,1024]{2,1,0:T(8,128)(2,1)}, bf16[16,1024]{1,0:T(8,128)(2,1)}) custom-call(s32[3]{0:T(128)S(1)} %copy-done.6, bf16[8,32,1024]{2,1,0:T(8,128)(2,1)S(1)} %all-to-all-done.pack_ref, bf16[16,1024]{1,0:T(8,128)(2,1)S(1)} %collective-permute-done.24.in_ref, bf16[1024,1024]{1,0:T(8,128)(2,1)} %bitcast.12.weight_ref.rest_0_, ...), custom_call_target="tpu_custom_call" | custom-call | flops 536870912 | bytes 16777216 | tf_op jit(solution)/shard_map/chain/pallas_call | solution.py:183
  290.6 6.4 %all-to-all-start.1 = ((bf16[8,32,1024]{2,1,0:T(8,128)(2,1)}), bf16[8,32,1024]{2,1,0:T(8,128)(2,1)S(1)}, u32[]{:S(2)}, u32[]{:S(2)}) async-start(bf16[8,32,1024]{2,1,0:T(8,128)(2,1)} %get-tuple-element.40), calls=%async_computation.1 | async-start | bytes 1048576 | tf_op jit(solution)/shard_map/all_to_all | solution.py:356
  301.2 5.2 %all-to-all-done.1.spread_ref = bf16[8,32,1024]{2,1,0:T(8,128)(2,1)S(1)} async-done(((bf16[8,32,1024]{2,1,0:T(8,128)(2,1)}), bf16[8,32,1024]{2,1,0:T(8,128)(2,1)S(1)}, u32[]{:S(2)}, u32[]{:S(2)}) %all-to-all-start.1) | async-done | bytes 524320 | tf_op jit(solution)/shard_map/all_to_all | solution.py:356
  307.2 9.7 %correct.1 = (bf16[4,128,512]{2,1,0:T(8,128)(2,1)}, bf16[4,1024,512]{2,1,0:T(8,128)(2,1)}) custom-call(s32[3]{0:T(128)} %pad_add_fusion.place_ref, bf16[8,32,1024]{2,1,0:T(8,128)(2,1)} %copy-done.8, bf16[4,128,1024]{2,1,0:T(8,128)(2,1)} %states_ref.9, f32[3,128,512]{2,1,0:T(8,128)} %slopes.3.slope_ref.slope_a, f32[3,128,512]{2,1,0:T(8,128)} %slopes.5.slope_b, ...), custom_call_target="tpu_custom_call" | custom-call | tf_op jit(solution)/shard_map/correct/pallas_call | solution.py:254
  317.0 56.3 %reduce-scatter.2.cloned.1.call-done = bf16[4,128,512]{2,1,0:T(8,128)(2,1)} async-done(((bf16[4,1024,512]{2,1,0:T(8,128)(2,1)}), bf16[4,128,512]{2,1,0:T(8,128)(2,1)}) %reduce-scatter.2.cloned.1.call-update) | async-done | bytes 524304 | tf_op jit(solution)/shard_map/reduce_scatter | solution.py:361
  (95 shorter events, 104.9 us)
Async XLA Ops:
  7.2 131.1 %all-gather.3.cloned.1.call-start = ((), (), s32[]{:S(2)}) async-start(), calls=%async_computation.3 | async-start | bytes 3538944 | tf_op jit(solution)/shard_map/all_gather | solution.py:319
  9.0 288.0 %all-gather.5.cloned.1.call-start = ((), (), s32[]{:S(2)}) async-start(), calls=%async_computation.4 | async-start | bytes 3538944 | tf_op jit(solution)/shard_map/all_gather | solution.py:327
  10.0 15.3 %collective-permute-start = (bf16[128,512]{1,0:T(8,128)(2,1)S(1)}, bf16[128,512]{1,0:T(8,128)(2,1)S(1)}, u32[]{:S(2)}, u32[]{:S(2)}) collective-permute-start(bf16[128,512]{1,0:T(8,128)(2,1)S(1)} %get-tuple-element.45), channel_id=1, source_target_pairs={{0,1},{1,0},{2,3},{3,2},{4,5},{5,4},{6,7},{7,6},{8,9},{9,8},{10,11... | collective-permute-start | bytes 393224 | tf_op jit(solution)/shard_map/ppermute | solution.py:23
  25.4 17.2 %collective-permute-start.1 = (bf16[128,1024]{1,0:T(8,128)(2,1)S(1)}, bf16[128,1024]{1,0:T(8,128)(2,1)S(1)}, u32[]{:S(2)}, u32[]{:S(2)}) collective-permute-start(bf16[128,1024]{1,0:T(8,128)(2,1)S(1)} %maximum_select_fusion.1), channel_id=1, source_target_pairs={{0,2},{2,4},{4,6},{6,8},{8,10},{10,12},{12,14},{14,0},{1,3},{3,5},... | collective-permute-start | bytes 786440 | tf_op jit(solution)/shard_map/ppermute | solution.py:28
  27.9 16.6 %collective-permute-start.2 = (bf16[128,1024]{1,0:T(8,128)(2,1)S(1)}, bf16[128,1024]{1,0:T(8,128)(2,1)S(1)}, u32[]{:S(2)}, u32[]{:S(2)}) collective-permute-start(bf16[128,1024]{1,0:T(8,128)(2,1)S(1)} %maximum_select_fusion.1), channel_id=1, source_target_pairs={{0,14},{2,0},{4,2},{6,4},{8,6},{10,8},{12,10},{14,12},{1,15},{3,1}... | collective-permute-start | bytes 786440 | tf_op jit(solution)/shard_map/ppermute | solution.py:28
  31.9 18.6 %collective-permute-start.5 = (bf16[3,128,512]{2,1,0:T(8,128)(2,1)}, bf16[3,128,512]{2,1,0:T(8,128)(2,1)S(1)}, u32[]{:S(2)}, u32[]{:S(2)}) collective-permute-start(bf16[3,128,512]{2,1,0:T(8,128)(2,1)} %slice.21), channel_id=1, source_target_pairs={{0,1},{1,0},{2,3},{3,2},{4,5},{5,4},{6,7},{7,6},{8,9},{9,8},{10,11... | collective-permute-start | bytes 1179656 | tf_op jit(solution)/shard_map/ppermute | solution.py:23
  42.6 16.0 %collective-permute-start.3 = (bf16[128,1024]{1,0:T(8,128)(2,1)S(1)}, bf16[128,1024]{1,0:T(8,128)(2,1)S(1)}, u32[]{:S(2)}, u32[]{:S(2)}) collective-permute-start(bf16[128,1024]{1,0:T(8,128)(2,1)S(1)} %collective-permute-done.1), channel_id=1, source_target_pairs={{0,2},{2,4},{4,6},{6,8},{8,10},{10,12},{12,14},{14,0},{1,3},{3,5},... | collective-permute-start | bytes 786440 | tf_op jit(solution)/shard_map/ppermute | solution.py:28
  44.5 14.8 %collective-permute-start.4 = (bf16[128,1024]{1,0:T(8,128)(2,1)S(1)}, bf16[128,1024]{1,0:T(8,128)(2,1)S(1)}, u32[]{:S(2)}, u32[]{:S(2)}) collective-permute-start(bf16[128,1024]{1,0:T(8,128)(2,1)S(1)} %collective-permute-done.2), channel_id=1, source_target_pairs={{0,14},{2,0},{4,2},{6,4},{8,6},{10,8},{12,10},{14,12},{1,15},{3,1}... | collective-permute-start | bytes 786440 | tf_op jit(solution)/shard_map/ppermute | solution.py:28
  59.3 16.4 %collective-permute-start.6 = (bf16[128,1024]{1,0:T(8,128)(2,1)S(1)}, bf16[128,1024]{1,0:T(8,128)(2,1)S(1)}, u32[]{:S(2)}, u32[]{:S(2)}) collective-permute-start(bf16[128,1024]{1,0:T(8,128)(2,1)S(1)} %collective-permute-done.3), channel_id=1, source_target_pairs={{0,2},{2,4},{4,6},{6,8},{8,10},{10,12},{12,14},{14,0},{1,3},{3,5},... | collective-permute-start | bytes 786440 | tf_op jit(solution)/shard_map/ppermute | solution.py:28
  61.9 15.8 %collective-permute-start.7 = (bf16[128,1024]{1,0:T(8,128)(2,1)S(1)}, bf16[128,1024]{1,0:T(8,128)(2,1)S(1)}, u32[]{:S(2)}, u32[]{:S(2)}) collective-permute-start(bf16[128,1024]{1,0:T(8,128)(2,1)S(1)} %collective-permute-done.4), channel_id=1, source_target_pairs={{0,14},{2,0},{4,2},{6,4},{8,6},{10,8},{12,10},{14,12},{1,15},{3,1}... | collective-permute-start | bytes 786440 | tf_op jit(solution)/shard_map/ppermute | solution.py:28
  84.9 95.2 %collective-permute-start.10 = (bf16[1024,1024]{1,0:T(8,128)(2,1)}, bf16[1024,1024]{1,0:T(8,128)(2,1)}, u32[]{:S(2)}, u32[]{:S(2)}) collective-permute-start(bf16[1024,1024]{1,0:T(8,128)(2,1)} %bitcast.12.weight_ref.rest_0_), channel_id=1, source_target_pairs={{0,96},{32,0},{64,32},{96,64},{1,97},{33,1},{65,33},{97,65},{2,98}... | collective-permute-start | bytes 6291464 | tf_op jit(solution)/shard_map/ppermute | solution.py:28
  87.3 92.7 %collective-permute-start.11 = (bf16[1024,1024]{1,0:T(8,128)(2,1)}, bf16[1024,1024]{1,0:T(8,128)(2,1)}, u32[]{:S(2)}, u32[]{:S(2)}) collective-permute-start(bf16[1024,1024]{1,0:T(8,128)(2,1)} %bitcast.12.weight_ref.rest_0_), channel_id=1, source_target_pairs={{0,32},{32,64},{64,96},{96,0},{1,33},{33,65},{65,97},{97,1},{2,34}... | collective-permute-start | bytes 6291464 | tf_op jit(solution)/shard_map/ppermute | solution.py:28
  90.2 47.3 %collective-permute-start.12 = (bf16[128,1024]{1,0:T(8,128)(2,1)S(1)}, bf16[128,1024]{1,0:T(8,128)(2,1)S(1)}, u32[]{:S(2)}, u32[]{:S(2)}) collective-permute-start(bf16[128,1024]{1,0:T(8,128)(2,1)S(1)} %bitcast.26), channel_id=1, source_target_pairs={{16,0},{32,16},{48,32},{64,48},{80,64},{96,80},{112,96},{128,112},... | collective-permute-start | bytes 786440 | tf_op jit(solution)/shard_map/ppermute | solution.py:328
  141.8 10.1 %collective-permute-start.13 = (bf16[128,512]{1,0:T(8,128)(2,1)}, bf16[128,512]{1,0:T(8,128)(2,1)S(1)}, u32[]{:S(2)}, u32[]{:S(2)}) collective-permute-start(bf16[128,512]{1,0:T(8,128)(2,1)} %get-tuple-element.26), channel_id=1, source_target_pairs={{0,1},{1,0},{2,3},{3,2},{4,5},{5,4},{6,7},{7,6},{8,9},{9,8},{10,11... | collective-permute-start | bytes 393224 | tf_op jit(solution)/shard_map/ppermute | solution.py:23
  154.1 9.6 %collective-permute-start.14 = (bf16[128,512]{1,0:T(8,128)(2,1)S(1)}, bf16[128,512]{1,0:T(8,128)(2,1)S(1)}, u32[]{:S(2)}, u32[]{:S(2)}) collective-permute-start(bf16[128,512]{1,0:T(8,128)(2,1)S(1)} %get-tuple-element.28), channel_id=1, source_target_pairs={{0,1},{1,0},{2,3},{3,2},{4,5},{5,4},{6,7},{7,6},{8,9},{9,8},{10,11... | collective-permute-start | bytes 393224 | tf_op jit(solution)/shard_map/ppermute | solution.py:23
  164.8 11.0 %collective-permute-start.15 = (bf16[128,1024]{1,0:T(8,128)(2,1)S(1)}, bf16[128,1024]{1,0:T(8,128)(2,1)S(1)}, u32[]{:S(2)}, u32[]{:S(2)}) collective-permute-start(bf16[128,1024]{1,0:T(8,128)(2,1)S(1)} %get-tuple-element.30), channel_id=1, source_target_pairs={{0,1},{1,0},{2,3},{3,2},{4,5},{5,4},{6,7},{7,6},{8,9},{9,8},{10,11... | collective-permute-start | bytes 786440 | tf_op jit(solution)/shard_map/ppermute | solution.py:23
  182.3 41.8 %collective-permute-start.16 = (bf16[512,1024]{1,0:T(8,128)(2,1)}, bf16[512,1024]{1,0:T(8,128)(2,1)}, u32[]{:S(2)}, u32[]{:S(2)}) collective-permute-start(bf16[512,1024]{1,0:T(8,128)(2,1)} %slice.24), channel_id=1, source_target_pairs={{0,96},{32,0},{64,32},{96,64},{1,97},{33,1},{65,33},{97,65},{2,98}... | collective-permute-start | bytes 3145736 | tf_op jit(solution)/shard_map/ppermute | solution.py:28
  186.5 37.6 %collective-permute-start.17 = (bf16[512,1024]{1,0:T(8,128)(2,1)}, bf16[512,1024]{1,0:T(8,128)(2,1)}, u32[]{:S(2)}, u32[]{:S(2)}) collective-permute-start(bf16[512,1024]{1,0:T(8,128)(2,1)} %slice.25), channel_id=1, source_target_pairs={{0,32},{32,64},{64,96},{96,0},{1,33},{33,65},{65,97},{97,1},{2,34}... | collective-permute-start | bytes 3145736 | tf_op jit(solution)/shard_map/ppermute | solution.py:28
  190.9 33.2 %all-to-all-start = ((bf16[8,32,1024]{2,1,0:T(8,128)(2,1)}), bf16[8,32,1024]{2,1,0:T(8,128)(2,1)S(1)}, u32[]{:S(2)}, u32[]{:S(2)}) async-start(bf16[8,32,1024]{2,1,0:T(8,128)(2,1)} %last_step.1), calls=%async_computation | async-start | bytes 1048576 | tf_op jit(solution)/shard_map/all_to_all | solution.py:343
  198.3 31.7 %collective-permute-start.18 = (bf16[1024,1024]{1,0:T(8,128)(2,1)}, bf16[1024,1024]{1,0:T(8,128)(2,1)S(1)}, u32[]{:S(2)}, u32[]{:S(2)}) collective-permute-start(bf16[1024,1024]{1,0:T(8,128)(2,1)} %bitcast.12.weight_ref.rest_0_), channel_id=1, source_target_pairs={{0,16},{16,0},{1,17},{17,1},{2,18},{18,2},{3,19},{19,3},{4,20},{20... | collective-permute-start | bytes 6291464 | tf_op jit(solution)/shard_map/ppermute | solution.py:23
  200.2 29.8 %collective-permute-start.19 = (bf16[1024,1024]{1,0:T(8,128)(2,1)}, bf16[1024,1024]{1,0:T(8,128)(2,1)}, u32[]{:S(2)}, u32[]{:S(2)}) collective-permute-start(bf16[1024,1024]{1,0:T(8,128)(2,1)} %collective-permute-done.10.rest_1_), channel_id=1, source_target_pairs={{0,16},{16,0},{1,17},{17,1},{2,18},{18,2},{3,19},{19,3},{4,20},{20... | collective-permute-start | bytes 6291464 | tf_op jit(solution)/shard_map/ppermute | solution.py:23
  202.6 27.4 %collective-permute-start.21 = (bf16[1024,1024]{1,0:T(8,128)(2,1)}, bf16[1024,1024]{1,0:T(8,128)(2,1)}, u32[]{:S(2)}, u32[]{:S(2)}) collective-permute-start(bf16[1024,1024]{1,0:T(8,128)(2,1)} %collective-permute-done.11.rest_3_), channel_id=1, source_target_pairs={{0,16},{16,0},{1,17},{17,1},{2,18},{18,2},{3,19},{19,3},{4,20},{20... | collective-permute-start | bytes 6291464 | tf_op jit(solution)/shard_map/ppermute | solution.py:23
  290.6 15.8 %all-to-all-start.1 = ((bf16[8,32,1024]{2,1,0:T(8,128)(2,1)}), bf16[8,32,1024]{2,1,0:T(8,128)(2,1)S(1)}, u32[]{:S(2)}, u32[]{:S(2)}) async-start(bf16[8,32,1024]{2,1,0:T(8,128)(2,1)} %get-tuple-element.40), calls=%async_computation.1 | async-start | bytes 1048576 | tf_op jit(solution)/shard_map/all_to_all | solution.py:356
  297.0 76.3 %reduce-scatter.2.cloned.1.call-start = ((), (), s32[]{:S(2)}) async-start(), calls=%async_computation.5 | async-start | bytes 4718592 | tf_op jit(solution)/shard_map/reduce_scatter | solution.py:361
  (17 other events, 256.5 us)
Sparse Core Ops, SparseCore 0:
  10.6 65.6 all-gather.2
  90.3 52.2 all-gather.4
  317.1 56.1 reduce-scatter.1

commit v3 on v2

v3 whole, which is shorter than its diff:
```python
import functools

import jax
import jax.numpy as jnp
from jax import lax
from jax.experimental import pallas as pl
from jax.experimental.pallas import tpu as pltpu
from jax.sharding import Mesh
from jax.sharding import PartitionSpec as P

step_size = 0.1
BF = jnp.bfloat16
F32 = jnp.float32
LAYER = ("zl", "x", "core")
RING = ("x", "core")


def back_product(scaled, weight):
    return lax.dot_general(scaled, weight, (((1,), (1,)), ((), ())), preferred_element_type=F32)


def swapped(value, axis):
    return lax.ppermute(value, axis, [(0, 1), (1, 0)])


def rotated(value, axis, steps):
    count = lax.axis_size(axis)
    return lax.ppermute(value, axis, [(i, (i + steps) % count) for i in range(count)])


def halves(value, index):
    half = value.shape[1] // 2
    low, high = value[:, :half], value[:, half:]
    return jnp.where(index == 0, low, high), jnp.where(index == 0, high, low)


def params(mib):
    return pltpu.CompilerParams(vmem_limit_bytes=mib * 2**20)


def cost(flops, moved):
    return pl.CostEstimate(flops=flops, bytes_accessed=moved, transcendentals=0)


def relax_kernel(
    blocks, place_ref, states_ref, own_ref, far_ref, far_low_ref, term_ref, guess_ref,
    slope_own, slope_far, pack_ref, v_own, v_far,
):
    turn = pl.program_id(0)
    last = pl.num_programs(0) - 1
    rows, width = term_ref.shape

    @pl.when(turn == 0)
    def _():
        v_own[...], v_far[...] = halves(term_ref[...].astype(F32), place_ref[2])

    def part(weight, slope_ref, v_ref):
        tangent = jnp.tanh(jnp.dot(states_ref[0], weight, preferred_element_type=F32))
        slope = 1.0 - tangent * tangent
        slope_ref[0] = slope
        scaled = (v_ref[...] * slope).astype(BF)
        return slope, back_product(scaled, weight)

    def step(far):
        slope, product = part(own_ref[0], slope_own, v_own)
        slope_other, product_other = part(far, slope_far, v_far)
        own, other = halves(step_size * (product + product_other), place_ref[2])
        v_own[...] += own
        v_far[...] += other
        return slope, slope_other

    def joined(own, far):
        first = place_ref[2] == 0
        return jnp.concatenate([jnp.where(first, own, far), jnp.where(first, far, own)], 1)

    @pl.when(turn < last)
    def _():
        step(far_ref[0])

    @pl.when(turn == last)
    def _():
        slope = joined(*step(far_low_ref[...]))
        residual = joined(v_own[...], v_far[...]) - guess_ref[...].astype(F32)
        size = rows // blocks
        pack_ref[:, :size, :] = residual.astype(BF).reshape(blocks, size, width)
        pack_ref[:, size:, :] = slope.astype(BF).reshape(blocks, size, width)


def relax(place, states, own, far, far_low, terminal, guess, blocks):
    layers, rows, width = states.shape
    half = width // 2
    top = layers - 1
    layer = lambda t, place: (top - t, 0, 0)
    whole = lambda v: pl.BlockSpec(v.shape, lambda t, place: (0,) * v.ndim)
    pack = jax.ShapeDtypeStruct((blocks, 2 * rows // blocks, width), BF)
    slopes = jax.ShapeDtypeStruct((layers, rows, half), F32)
    return pl.pallas_call(
        functools.partial(relax_kernel, blocks),
        grid_spec=pltpu.PrefetchScalarGridSpec(
            num_scalar_prefetch=1,
            grid=(layers,),
            in_specs=[
                pl.BlockSpec((1, rows, width), layer),
                pl.BlockSpec((1, width, half), layer),
                pl.BlockSpec((1, width, half), lambda t, place: (jnp.maximum(top - 1 - t, 0), 0, 0)),
                whole(far_low),
                whole(terminal),
                whole(guess),
            ],
            out_specs=[
                pl.BlockSpec((1, rows, half), layer),
                pl.BlockSpec((1, rows, half), layer),
                whole(pack),
            ],
            scratch_shapes=[pltpu.VMEM((rows, half), F32)] * 2,
        ),
        out_shape=[slopes, slopes, pack],
        compiler_params=params(56),
        cost_estimate=cost(4 * layers * rows * width * width, 2 * layers * width * width),
        name="relax",
    )(place, states, own, far, far_low, terminal, guess)


def chain_kernel(chips, place_ref, pack_ref, in_ref, *rest):
    mine, other, (out_ref, low_ref, held, arrived) = rest[:5], rest[5:10], rest[10:]
    count = 2 * chips
    part = in_ref.shape[0]
    scale = 4 * step_size

    def fetch(source, point, side):
        return pltpu.make_async_copy(source, held.at[point, side], arrived.at[point, side])

    def source_of(group, hop, side):
        here, ahead, behind, front, back = group
        if hop == 2:
            return (front, back)[side]
        return (here, ahead, None, behind)[hop].at[side]

    for point in range(count - 1, -1, -1):
        distance = lax.rem(point // 2 - place_ref[0] + chips, chips)
        same = place_ref[1] == point % 2
        for hop in range(chips):
            @pl.when((distance == hop) & same)
            def _():
                for side in range(2):
                    fetch(source_of(mine, hop, side), point, side).start()

            @pl.when((distance == hop) & jnp.logical_not(same))
            def _():
                for side in range(2):
                    fetch(source_of(other, hop, side), point, side).start()

    short = in_ref[...]
    for point in range(count - 1, -1, -1):
        v = short.astype(F32)
        scaled = (v * pack_ref[point, part:, :].astype(F32)).astype(BF)
        out_ref[point, :part, :] = short
        base = v + pack_ref[point, :part, :].astype(F32)
        own, far = halves(scaled, place_ref[2])
        fetch(mine[3], point, 0).wait()
        product = back_product(own, held[point, 0])
        fetch(mine[3], point, 1).wait()
        product += back_product(far, held[point, 1])
        short = (base + scale * product).astype(BF)
        out_ref[point, part:, :] = short
    low_ref[...] = short


def chain(place, pack, sources, incoming):
    chips = lax.axis_size("x")
    weight = sources[0].shape
    whole = lambda v: pl.BlockSpec(v.shape, lambda t, place: (0,) * v.ndim)
    return pl.pallas_call(
        functools.partial(chain_kernel, chips),
        grid_spec=pltpu.PrefetchScalarGridSpec(
            num_scalar_prefetch=1,
            grid=(1,),
            in_specs=[whole(pack), whole(incoming)]
            + [pl.BlockSpec(memory_space=pl.ANY)] * len(sources),
            out_specs=[whole(pack), whole(incoming)],
            scratch_shapes=[
                pltpu.VMEM((2 * chips,) + weight, BF),
                pltpu.SemaphoreType.DMA((2 * chips, 2)),
            ],
        ),
        out_shape=[
            jax.ShapeDtypeStruct(pack.shape, BF),
            jax.ShapeDtypeStruct(incoming.shape, BF),
        ],
        compiler_params=params(40),
        cost_estimate=cost(2 * pack.size * weight[1], 8 * chips * weight[1] ** 2),
        name="chain",
    )(place, pack, incoming, *sources)


def correct_kernel(
    place_ref, spread_ref, states_ref, slope_a, slope_b, weight_a, weight_b,
    term_ref, guess_ref, adj_ref, part_ref, own_ref, other_ref,
):
    turn = pl.program_id(0)
    last = pl.num_programs(0) - 1
    rows, width = term_ref.shape
    part = spread_ref.shape[1] // 2

    def split(value):
        return halves(value, place_ref[2])

    def terms(scaled):
        product = lax.dot_general(
            states_ref[0], scaled, (((0,), (0,)), ((), ())), preferred_element_type=F32
        )
        part_ref[0] = product.astype(BF)

    @pl.when(turn == 0)
    def _():
        error = spread_ref[:, :part, :].reshape(rows, width).astype(F32)
        own_ref[...], other_ref[...] = split(term_ref[...].astype(F32) + error)

    @pl.when(turn < last)
    def _():
        scaled = (own_ref[...] * slope_a[0]).astype(BF)
        scaled_other = (other_ref[...] * slope_b[0]).astype(BF)
        terms(scaled)
        product = back_product(scaled, weight_a[0]) + back_product(scaled_other, weight_b[0])
        own, other = split(step_size * product)
        current = own_ref[...] + own
        own_ref[...] = current
        other_ref[...] += other
        adj_ref[0] = current.astype(BF)

    @pl.when(turn == last)
    def _():
        terms((own_ref[...] * slope_a[0]).astype(BF))
        error = spread_ref[:, part:, :].reshape(rows, width).astype(F32)
        adj_ref[0] = split(guess_ref[...].astype(F32) + error)[0].astype(BF)


def correct(place, spread, states, slopes_a, slopes_b, weights_a, weights_b, terminal, guess):
    layers, rows, width = states.shape
    half = width // 2
    top = layers - 1
    lower = lambda t, place: (jnp.maximum(top - 1 - t, 0), 0, 0)
    whole = lambda v: pl.BlockSpec(v.shape, lambda t, place: (0,) * v.ndim)
    layer = lambda v: pl.BlockSpec((1,) + v.shape[1:], lambda t, place: (top - t, 0, 0))
    return pl.pallas_call(
        correct_kernel,
        grid_spec=pltpu.PrefetchScalarGridSpec(
            num_scalar_prefetch=1,
            grid=(layers,),
            in_specs=[
                whole(spread),
                pl.BlockSpec((1, rows, width), lambda t, place: (top - t, 0, 0)),
                layer(slopes_a),
                layer(slopes_b),
                layer(weights_a),
                pl.BlockSpec((1, width, half), lower),
                whole(terminal),
                whole(guess),
            ],
            out_specs=[
                pl.BlockSpec((1, rows, half), lambda t, place: (top - t, 0, 0)),
                pl.BlockSpec((1, width, half), lambda t, place: (top - t, 0, 0)),
            ],
            scratch_shapes=[pltpu.VMEM((rows, half), F32)] * 2,
        ),
        out_shape=[
            jax.ShapeDtypeStruct((layers, rows, half), BF),
            jax.ShapeDtypeStruct((layers, width, half), BF),
        ],
        compiler_params=params(56),
        name="correct",
    )(place, spread, states, slopes_a, slopes_b, weights_a, weights_b, terminal, guess)


def put(buffer, value, *index):
    lead = len(index)
    start = tuple(index) + (0,) * (buffer.ndim - lead)
    return lax.dynamic_update_slice(buffer, value.reshape((1,) * lead + value.shape), start)


def ring_gather(piece, beside):
    count = lax.axis_size("dp")
    me = lax.axis_index("dp")
    rows = piece.shape[0]
    mid = rows // 2
    whole = put(jnp.zeros((count,) + piece.shape, piece.dtype), piece, me)
    up = down = piece
    for hop in range(1, count // 2):
        if hop == count // 2 - 1:
            up, down, beside = lax.optimization_barrier((up, down, beside))
        up, down = rotated(up, "dp", 1), rotated(down, "dp", -1)
        whole = put(whole, up, (me - hop) % count)
        whole = put(whole, down, (me + hop) % count)
    far = jnp.concatenate([rotated(up[:mid], "dp", 1), rotated(down[mid:], "dp", -1)], 0)
    whole = put(whole, far, (me + count // 2) % count)
    return whole.reshape((count * rows,) + piece.shape[1:]), beside


def body(states, weights, guess_points, cotangent):
    slabs = lax.axis_size(LAYER)
    slab = lax.axis_index(LAYER)
    half_index = lax.axis_index("mp")
    place = jnp.stack([lax.axis_index("x"), lax.axis_index("core"), half_index]).astype(jnp.int32)
    blocks = lax.axis_size(RING)
    layers, rows, width = states.shape
    guess = guess_points[0]

    own = lax.all_gather(weights, "dp", axis=1, tiled=True)
    next_guess = lax.ppermute(guess, LAYER, [(i, i - 1) for i in range(1, slabs)])
    far_low, (shards, next_guess) = ring_gather(
        swapped(weights[0], "mp"), (swapped(weights[1:], "mp"), next_guess)
    )
    far = lax.all_gather(shards, "dp", axis=1, tiled=True)
    terminal = jnp.where(slab == slabs - 1, cotangent, next_guess)

    here = jnp.stack([own[0], far_low])
    ahead = rotated(here, "x", -1)
    behind = rotated(here, "x", 1)
    front, back = rotated(ahead[0], "x", -1), rotated(behind[1], "x", 1)

    slopes_own, slopes_far, pack = relax(
        place, states, own, far, far_low, terminal, guess, blocks
    )
    pack = lax.all_to_all(pack, RING, 0, 0, tiled=True)
    front, back, pack = lax.optimization_barrier((front, back, pack))
    ring = (here, ahead, behind, front, back)
    ring = ring + tuple(swapped(value, "core") for value in ring)

    incoming = jnp.zeros((pack.shape[1] // 2, width), BF)
    stages = lax.axis_size("zl")
    for stage in range(stages):
        errors, lowest = chain(place, pack, ring, incoming)
        if stage < stages - 1:
            incoming = lax.ppermute(lowest, "zl", [(i, i - 1) for i in range(1, stages)])
    spread = lax.all_to_all(errors, RING, 0, 0, tiled=True)

    adjoint, partial = correct(
        place, spread, states, slopes_own, slopes_far, own, far, terminal, guess
    )
    grads = lax.psum_scatter(partial, "dp", scatter_dimension=1, tiled=True)
    return adjoint, step_size * grads.astype(F32)


def solution(mesh):
    slabs, rows, halves = (mesh.shape[name] for name in ("layer", "dp", "mp"))
    fine = Mesh(
        mesh.devices.reshape(slabs // 8, 4, 2, rows, halves), ("zl", "x", "core", "dp", "mp")
    )
    return jax.shard_map(
        body,
        mesh=fine,
        in_specs=(
            P(LAYER, "dp", None),
            P(LAYER, "dp", "mp"),
            P(LAYER, "dp", None),
            P("dp", None),
        ),
        out_specs=(P(LAYER, "dp", "mp"), P(LAYER, "dp", "mp")),
        check_vma=False,
    )
```

time: 384 us -> 325 us (0.85)
  starting transfers between devices: 107 us -> 73.1 us
  waiting for transfers between devices: 172 us -> 140 us
  blocking collectives: 0 us -> 28.5 us
  local copies, waits for them, and re-layouts: 20 us -> 9.41 us
  Pallas kernels: 63.4 us -> 54.6 us
    ppermute x12, waiting for transfers between devices: 16.9 us -> 64 us  [rotated(): lax.ppermute(value, axis, [(i, (i + steps) % count) for i in range(count)])]
    ppermute x1, waiting for transfers between devices: 40.2 us -> 0.01 us  [body(): lax.ppermute(guess, LAYER, [(i, i - 1) for i in range(1, slabs)])]
    all_to_all x0 -> x2, blocking collectives: none -> 28.5 us  [the longest x1 15.8 us: body(): spread = lax.all_to_all(errors, RING, 0, 0, tiled=True)]
    all_to_all x2 -> x0, waiting for transfers between devices: 24.7 us -> none  [the longest x1 19.5 us: body(): pack = lax.all_to_all(pack, RING, 0, 0, tiled=True)]
    ppermute x9 -> x7, starting transfers between devices: 44.5 us -> 26.7 us  [swapped(): return lax.ppermute(value, axis, [(0, 1), (1, 0)])]
    all_to_all x2 -> x0, starting transfers between devices: 13.8 us -> none  [the longest x1 7.39 us: body(): pack = lax.all_to_all(pack, RING, 0, 0, tiled=True)]
    ppermute x9 -> x7, waiting for transfers between devices: 15.8 us -> 3.55 us  [swapped(): return lax.ppermute(value, axis, [(0, 1), (1, 0)])]
    pallas_call x11 -> x5, Pallas kernels: 53.6 us -> 45 us  [the longest x4 35.2 us: chain(): pl.pallas_call(functools.partial(chain_kernel, chips), grid_spec=pltpu.Pr...]
  transfers between devices with their start and end apart: 30 -> 26, of which waited for: 16 -> 14; matrix products, arithmetic and copies ran while one was open for 4% -> 3% of each run, Pallas kernels for 14% -> 3%
where the time goes in v3:
time: 325 us; the launch traced here: 324 us
  waiting for transfers between devices  140 us (43%)
  starting transfers between devices  73.1 us (22%)
  Pallas kernels  54.6 us (17%)
  blocking collectives  28.5 us (9%)
  between operations  14.3 us (4%)
  local copies, waits for them, and re-layouts  9.41 us (3%)
  other arithmetic  4.65 us (1%)
    ppermute x12, waiting for transfers between devices, rotated(): lax.ppermute(value, axis, [(i, (i + steps) % count) for i in range(count)])  64 us
    reduce_scatter x1, waiting for transfers between devices, body(): grads = lax.psum_scatter(partial, 'dp', scatter_dimension=1, tiled=True)  55.4 us
    ppermute x12, starting transfers between devices, rotated(): lax.ppermute(value, axis, [(i, (i + steps) % count) for i in range(count)])  38.9 us
    pallas_call x4, Pallas kernels, chain(): pl.pallas_call(functools.partial(chain_kernel, chips), grid_spec=pltpu.Pr...  35.2 us
    ppermute x7, starting transfers between devices, swapped(): return lax.ppermute(value, axis, [(0, 1), (1, 0)])  26.7 us
    all_to_all x1, blocking collectives, body(): spread = lax.all_to_all(errors, RING, 0, 0, tiled=True)  15.8 us
    all_to_all x1, blocking collectives, body(): pack = lax.all_to_all(pack, RING, 0, 0, tiled=True)  12.7 us
    ppermute x3, waiting for transfers between devices, body(): lax.ppermute(lowest, 'zl', [(i, i - 1) for i in range(1, stages)])  10.2 us
  transfers between devices with their start and end apart: 26, of which 14 were waited for; matrix products, arithmetic and copies ran while one was open for 3% of the time, Pallas kernels for 3%

profile of v3, /device:TPU:1, one launch (start us, length us, event | category | flops | bytes accessed | tf_op | source)
XLA Modules:
  0.0 324.3 jit_solution(1560585211125246616)
XLA Ops:
  8.9 11.5 %collective-permute-start = (bf16[128,512]{1,0:T(8,128)(2,1)S(1)}, bf16[128,512]{1,0:T(8,128)(2,1)S(1)}, u32[]{:S(2)}, u32[]{:S(2)}) collective-permute-start(bf16[128,512]{1,0:T(8,128)(2,1)S(1)} %slice_bitcast_fusion.2), channel_id=1, source_target_pairs={{0,1},{1,0},{2,3},{3,2},{4,5},{5,4},{6,7},{7,6},{8,9},{9,8},{10,11... | collective-permute-start | bytes 393224 | tf_op jit(solution)/shard_map/ppermute | solution.py:23
  24.2 4.4 %collective-permute-start.2 = (bf16[128,512]{1,0:T(8,128)(2,1)S(1)}, bf16[128,512]{1,0:T(8,128)(2,1)S(1)}, u32[]{:S(2)}, u32[]{:S(2)}) collective-permute-start(bf16[128,512]{1,0:T(8,128)(2,1)S(1)} %collective-permute-done), channel_id=1, source_target_pairs={{0,14},{2,0},{4,2},{6,4},{8,6},{10,8},{12,10},{14,12},{1,15},{3,1}... | collective-permute-start | bytes 393224 | tf_op jit(solution)/shard_map/ppermute | solution.py:28
  28.6 3.5 %collective-permute-start.6 = (bf16[128,1024]{1,0:T(8,128)(2,1)}, bf16[128,1024]{1,0:T(8,128)(2,1)S(1)}, u32[]{:S(2)}, u32[]{:S(2)}) collective-permute-start(bf16[128,1024]{1,0:T(8,128)(2,1)} %bitcast.32), channel_id=1, source_target_pairs={{16,0},{32,16},{48,32},{64,48},{80,64},{96,80},{112,96},{128,112},... | collective-permute-start | bytes 786440 | tf_op jit(solution)/shard_map/ppermute | solution.py:309
  38.7 5.0 %collective-permute-done.1 = bf16[128,512]{1,0:T(8,128)(2,1)S(1)} collective-permute-done((bf16[128,512]{1,0:T(8,128)(2,1)S(1)}, bf16[128,512]{1,0:T(8,128)(2,1)S(1)}, u32[]{:S(2)}, u32[]{:S(2)}) %collective-permute-start.1) | collective-permute-done | bytes 131104 | tf_op jit(solution)/shard_map/ppermute | solution.py:28
  46.3 8.8 %collective-permute-done.3 = bf16[128,512]{1,0:T(8,128)(2,1)S(1)} collective-permute-done((bf16[128,512]{1,0:T(8,128)(2,1)S(1)}, bf16[128,512]{1,0:T(8,128)(2,1)S(1)}, u32[]{:S(2)}, u32[]{:S(2)}) %collective-permute-start.3) | collective-permute-done | bytes 131104 | tf_op jit(solution)/shard_map/ppermute | solution.py:28
  58.2 4.6 %collective-permute-start.8 = (bf16[128,512]{1,0:T(8,128)(2,1)S(1)}, bf16[128,512]{1,0:T(8,128)(2,1)S(1)}, u32[]{:S(2)}, u32[]{:S(2)}) collective-permute-start(bf16[128,512]{1,0:T(8,128)(2,1)S(1)} %collective-permute-done.4), channel_id=1, source_target_pairs={{0,14},{2,0},{4,2},{6,4},{8,6},{10,8},{12,10},{14,12},{1,15},{3,1}... | collective-permute-start | bytes 393224 | tf_op jit(solution)/shard_map/ppermute | solution.py:28
  62.8 4.7 %collective-permute-done.7 = bf16[128,512]{1,0:T(8,128)(2,1)S(1)} collective-permute-done((bf16[128,512]{1,0:T(8,128)(2,1)S(1)}, bf16[128,512]{1,0:T(8,128)(2,1)S(1)}, u32[]{:S(2)}, u32[]{:S(2)}) %collective-permute-start.7) | collective-permute-done | bytes 131104 | tf_op jit(solution)/shard_map/ppermute | solution.py:28
  69.5 4.6 %collective-permute-start.10 = (bf16[64,512]{1,0:T(8,128)(2,1)S(1)}, bf16[64,512]{1,0:T(8,128)(2,1)S(1)}, u32[]{:S(2)}, u32[]{:S(2)}) collective-permute-start(bf16[64,512]{1,0:T(8,128)(2,1)S(1)} %slice.30), channel_id=1, source_target_pairs={{0,14},{2,0},{4,2},{6,4},{8,6},{10,8},{12,10},{14,12},{1,15},{3,1}... | collective-permute-start | bytes 196616 | tf_op jit(solution)/shard_map/ppermute | solution.py:28
  76.5 5.8 %all-gather.3.cloned.1.call-done.own_ref.weight_a = bf16[4,1024,512]{2,1,0:T(8,128)(2,1)} async-done(((bf16[4,128,512]{2,1,0:T(8,128)(2,1)}), bf16[4,1024,512]{2,1,0:T(8,128)(2,1)}) %all-gather.3.cloned.1.call-update) | async-done | bytes 4194320 | tf_op jit(solution)/shard_map/all_gather | solution.py:308
  87.0 3.4 %collective-permute-start.11 = (bf16[2,1024,512]{2,1,0:T(8,128)(2,1)S(1)}, bf16[2,1024,512]{2,1,0:T(8,128)(2,1)}, u32[]{:S(2)}, u32[]{:S(2)}) collective-permute-start(bf16[2,1024,512]{2,1,0:T(8,128)(2,1)S(1)} %pad_maximum_fusion.rest_0_), channel_id=1, source_target_pairs={{0,96},{32,0},{64,32},{96,64},{1,97},{33,1},{65,33},{97,65},{2,98}... | collective-permute-start | bytes 6291464 | tf_op jit(solution)/shard_map/ppermute | solution.py:28
  90.4 43.0 %collective-permute-done.13.rest_2_ = bf16[2,1024,512]{2,1,0:T(8,128)(2,1)} collective-permute-done((bf16[2,1024,512]{2,1,0:T(8,128)(2,1)S(1)}, bf16[2,1024,512]{2,1,0:T(8,128)(2,1)}, u32[]{:S(2)}, u32[]{:S(2)}) %collective-permute-start.13) | collective-permute-done | bytes 2097184 | tf_op jit(solution)/shard_map/ppermute | solution.py:28
  139.9 4.6 %collective-permute-start.12 = (bf16[1024,512]{1,0:T(8,128)(2,1)}, bf16[1024,512]{1,0:T(8,128)(2,1)}, u32[]{:S(2)}, u32[]{:S(2)}) collective-permute-start(bf16[1024,512]{1,0:T(8,128)(2,1)} %slice_bitcast_fusion.1), channel_id=1, source_target_pairs={{0,96},{32,0},{64,32},{96,64},{1,97},{33,1},{65,33},{97,65},{2,98}... | collective-permute-start | bytes 3145736 | tf_op jit(solution)/shard_map/ppermute | solution.py:28
  144.5 4.2 %collective-permute-start.15 = (bf16[2,1024,512]{2,1,0:T(8,128)(2,1)S(1)}, bf16[2,1024,512]{2,1,0:T(8,128)(2,1)}, u32[]{:S(2)}, u32[]{:S(2)}) collective-permute-start(bf16[2,1024,512]{2,1,0:T(8,128)(2,1)S(1)} %pad_maximum_fusion.rest_0_), channel_id=1, source_target_pairs={{0,16},{16,0},{1,17},{17,1},{2,18},{18,2},{3,19},{19,3},{4,20},{20... | collective-permute-start | bytes 6291464 | tf_op jit(solution)/shard_map/ppermute | solution.py:23
  155.3 9.8 %relax.1 = (f32[4,128,512]{2,1,0:T(8,128)}, f32[4,128,512]{2,1,0:T(8,128)}, bf16[8,32,1024]{2,1,0:T(8,128)(2,1)}) custom-call(s32[3]{0:T(128)} %pad_add_fusion.place_ref, bf16[4,128,1024]{2,1,0:T(8,128)(2,1)} %states_ref.3, bf16[4,1024,512]{2,1,0:T(8,128)(2,1)} %all-gather.3.cloned.1.call-done.own_ref.weight_a, ...), custom_call_target="tpu_custom_call" | custom-call | flops 2147483648 | bytes 8388608 | tf_op jit(solution)/shard_map/relax/pallas_call | solution.py:97
  165.2 12.7 %all_to_all.10.pack_ref = bf16[8,32,1024]{2,1,0:T(8,128)(2,1)S(1)} all-to-all(bf16[8,32,1024]{2,1,0:T(8,128)(2,1)} %get-tuple-element.22), channel_id=1, replica_groups=mesh['zl'=4,'x'=4,'core'=2,'dp'=8,'mp'=2] {'x','core'}, dimensions={0} | all-to-all | bytes 1048576 | tf_op jit(solution)/shard_map/all_to_all | solution.py:324
  185.4 8.8 %chain.4 = (bf16[8,32,1024]{2,1,0:T(8,128)(2,1)}, bf16[16,1024]{1,0:T(8,128)(2,1)S(1)}) custom-call(s32[3]{0:T(128)S(1)} %copy-done, bf16[8,32,1024]{2,1,0:T(8,128)(2,1)S(1)} %all_to_all.10.pack_ref, bf16[16,1024]{1,0:T(8,128)(2,1)S(1)} %broadcast_in_dim.7.in_ref, bf16[2,1024,512]{2,1,0:T(8,128)(2,1)S(1)} %pad_maximum_fusion.rest_0_, ...), custom_call_target="tpu_custom_call" | custom-call | flops 536870912 | bytes 33554432 | tf_op jit(solution)/shard_map/chain/pallas_call | solution.py:173
  198.9 8.8 %chain.5 = (bf16[8,32,1024]{2,1,0:T(8,128)(2,1)}, bf16[16,1024]{1,0:T(8,128)(2,1)S(1)}) custom-call(s32[3]{0:T(128)S(1)} %copy-done, bf16[8,32,1024]{2,1,0:T(8,128)(2,1)S(1)} %all_to_all.10.pack_ref, bf16[16,1024]{1,0:T(8,128)(2,1)S(1)} %collective-permute-done.20.in_ref, bf16[2,1024,512]{2,1,0:T(8,128)(2,1)S(1)} %pad_maximum_fusion.rest_0_, ...), custom_call_target="tpu_custom_call" | custom-call | flops 536870912 | bytes 33554432 | tf_op jit(solution)/shard_map/chain/pallas_call | solution.py:173
  209.1 3.5 %collective-permute-done.21.in_ref = bf16[16,1024]{1,0:T(8,128)(2,1)S(1)} collective-permute-done((bf16[16,1024]{1,0:T(8,128)(2,1)S(1)}, bf16[16,1024]{1,0:T(8,128)(2,1)S(1)}, u32[]{:S(2)}, u32[]{:S(2)}) %collective-permute-start.21) | collective-permute-done | bytes 32800 | tf_op jit(solution)/shard_map/ppermute | solution.py:334
  212.6 8.8 %chain.6 = (bf16[8,32,1024]{2,1,0:T(8,128)(2,1)}, bf16[16,1024]{1,0:T(8,128)(2,1)S(1)}) custom-call(s32[3]{0:T(128)S(1)} %copy-done, bf16[8,32,1024]{2,1,0:T(8,128)(2,1)S(1)} %all_to_all.10.pack_ref, bf16[16,1024]{1,0:T(8,128)(2,1)S(1)} %collective-permute-done.21.in_ref, bf16[2,1024,512]{2,1,0:T(8,128)(2,1)S(1)} %pad_maximum_fusion.rest_0_, ...), custom_call_target="tpu_custom_call" | custom-call | flops 536870912 | bytes 33554432 | tf_op jit(solution)/shard_map/chain/pallas_call | solution.py:173
  222.8 3.4 %collective-permute-done.22.in_ref = bf16[16,1024]{1,0:T(8,128)(2,1)S(1)} collective-permute-done((bf16[16,1024]{1,0:T(8,128)(2,1)S(1)}, bf16[16,1024]{1,0:T(8,128)(2,1)S(1)}, u32[]{:S(2)}, u32[]{:S(2)}) %collective-permute-start.22) | collective-permute-done | bytes 32800 | tf_op jit(solution)/shard_map/ppermute | solution.py:334
  226.1 8.7 %chain.7 = (bf16[8,32,1024]{2,1,0:T(8,128)(2,1)S(1)}, bf16[16,1024]{1,0:T(8,128)(2,1)}) custom-call(s32[3]{0:T(128)S(1)} %copy-done, bf16[8,32,1024]{2,1,0:T(8,128)(2,1)S(1)} %all_to_all.10.pack_ref, bf16[16,1024]{1,0:T(8,128)(2,1)S(1)} %collective-permute-done.22.in_ref, bf16[2,1024,512]{2,1,0:T(8,128)(2,1)S(1)} %pad_maximum_fusion.rest_0_, ...), custom_call_target="tpu_custom_call" | custom-call | flops 536870912 | bytes 33554432 | tf_op jit(solution)/shard_map/chain/pallas_call | solution.py:173
  234.8 15.8 %all_to_all.11.spread_ref = bf16[8,32,1024]{2,1,0:T(8,128)(2,1)} all-to-all(bf16[8,32,1024]{2,1,0:T(8,128)(2,1)S(1)} %get-tuple-element.29), channel_id=1, replica_groups=mesh['zl'=4,'x'=4,'core'=2,'dp'=8,'mp'=2] {'x','core'}, dimensions={0} | all-to-all | bytes 1048576 | tf_op jit(solution)/shard_map/all_to_all | solution.py:335
  250.6 9.6 %correct.1 = (bf16[4,128,512]{2,1,0:T(8,128)(2,1)}, bf16[4,1024,512]{2,1,0:T(8,128)(2,1)}) custom-call(s32[3]{0:T(128)} %pad_add_fusion.place_ref, bf16[8,32,1024]{2,1,0:T(8,128)(2,1)} %all_to_all.11.spread_ref, bf16[4,128,1024]{2,1,0:T(8,128)(2,1)} %states_ref.3, f32[4,128,512]{2,1,0:T(8,128)} %get-tuple-element.30.slope_a, ...), custom_call_target="tpu_custom_call" | custom-call | tf_op jit(solution)/shard_map/correct/pallas_call | solution.py:245
  260.2 55.4 %reduce-scatter.2.cloned.1.call-done = bf16[4,128,512]{2,1,0:T(8,128)(2,1)} async-done(((bf16[4,1024,512]{2,1,0:T(8,128)(2,1)}), bf16[4,128,512]{2,1,0:T(8,128)(2,1)}) %reduce-scatter.2.cloned.1.call-update) | async-done | bytes 524304 | tf_op jit(solution)/shard_map/reduce_scatter | solution.py:340
  (71 shorter events, 56.6 us)
Async XLA Ops:
  7.2 75.1 %all-gather.3.cloned.1.call-start = ((), (), s32[]{:S(2)}) async-start(), calls=%async_computation.3 | async-start | bytes 4718592 | tf_op jit(solution)/shard_map/all_gather | solution.py:308
  7.9 147.4 %all-gather.5.cloned.1.call-start = ((), (), s32[]{:S(2)}) async-start(), calls=%async_computation.4 | async-start | bytes 3538944 | tf_op jit(solution)/shard_map/all_gather | solution.py:313
  8.9 15.3 %collective-permute-start = (bf16[128,512]{1,0:T(8,128)(2,1)S(1)}, bf16[128,512]{1,0:T(8,128)(2,1)S(1)}, u32[]{:S(2)}, u32[]{:S(2)}) collective-permute-start(bf16[128,512]{1,0:T(8,128)(2,1)S(1)} %slice_bitcast_fusion.2), channel_id=1, source_target_pairs={{0,1},{1,0},{2,3},{3,2},{4,5},{5,4},{6,7},{7,6},{8,9},{9,8},{10,11... | collective-permute-start | bytes 393224 | tf_op jit(solution)/shard_map/ppermute | solution.py:23
  21.4 33.8 %collective-permute-start.5 = (bf16[3,128,512]{2,1,0:T(8,128)(2,1)S(1)}, bf16[3,128,512]{2,1,0:T(8,128)(2,1)S(1)}, u32[]{:S(2)}, u32[]{:S(2)}) collective-permute-start(bf16[3,128,512]{2,1,0:T(8,128)(2,1)S(1)} %slice.23), channel_id=1, source_target_pairs={{0,1},{1,0},{2,3},{3,2},{4,5},{5,4},{6,7},{7,6},{8,9},{9,8},{10,11... | collective-permute-start | bytes 1179656 | tf_op jit(solution)/shard_map/ppermute | solution.py:23
  24.2 11.1 %collective-permute-start.2 = (bf16[128,512]{1,0:T(8,128)(2,1)S(1)}, bf16[128,512]{1,0:T(8,128)(2,1)S(1)}, u32[]{:S(2)}, u32[]{:S(2)}) collective-permute-start(bf16[128,512]{1,0:T(8,128)(2,1)S(1)} %collective-permute-done), channel_id=1, source_target_pairs={{0,14},{2,0},{4,2},{6,4},{8,6},{10,8},{12,10},{14,12},{1,15},{3,1}... | collective-permute-start | bytes 393224 | tf_op jit(solution)/shard_map/ppermute | solution.py:28
  28.6 17.0 %collective-permute-start.6 = (bf16[128,1024]{1,0:T(8,128)(2,1)}, bf16[128,1024]{1,0:T(8,128)(2,1)S(1)}, u32[]{:S(2)}, u32[]{:S(2)}) collective-permute-start(bf16[128,1024]{1,0:T(8,128)(2,1)} %bitcast.32), channel_id=1, source_target_pairs={{16,0},{32,16},{48,32},{64,48},{80,64},{96,80},{112,96},{128,112},... | collective-permute-start | bytes 786440 | tf_op jit(solution)/shard_map/ppermute | solution.py:309
  32.2 11.5 %collective-permute-start.1 = (bf16[128,512]{1,0:T(8,128)(2,1)S(1)}, bf16[128,512]{1,0:T(8,128)(2,1)S(1)}, u32[]{:S(2)}, u32[]{:S(2)}) collective-permute-start(bf16[128,512]{1,0:T(8,128)(2,1)S(1)} %collective-permute-done), channel_id=1, source_target_pairs={{0,2},{2,4},{4,6},{6,8},{8,10},{10,12},{12,14},{14,0},{1,3},{3,5},... | collective-permute-start | bytes 393224 | tf_op jit(solution)/shard_map/ppermute | solution.py:28
  35.3 10.3 %collective-permute-start.4 = (bf16[128,512]{1,0:T(8,128)(2,1)S(1)}, bf16[128,512]{1,0:T(8,128)(2,1)S(1)}, u32[]{:S(2)}, u32[]{:S(2)}) collective-permute-start(bf16[128,512]{1,0:T(8,128)(2,1)S(1)} %collective-permute-done.2), channel_id=1, source_target_pairs={{0,14},{2,0},{4,2},{6,4},{8,6},{10,8},{12,10},{14,12},{1,15},{3,1}... | collective-permute-start | bytes 393224 | tf_op jit(solution)/shard_map/ppermute | solution.py:28
  43.7 11.4 %collective-permute-start.3 = (bf16[128,512]{1,0:T(8,128)(2,1)S(1)}, bf16[128,512]{1,0:T(8,128)(2,1)S(1)}, u32[]{:S(2)}, u32[]{:S(2)}) collective-permute-start(bf16[128,512]{1,0:T(8,128)(2,1)S(1)} %collective-permute-done.1), channel_id=1, source_target_pairs={{0,2},{2,4},{4,6},{6,8},{8,10},{10,12},{12,14},{14,0},{1,3},{3,5},... | collective-permute-start | bytes 393224 | tf_op jit(solution)/shard_map/ppermute | solution.py:28
  55.9 259.7 %reduce-scatter.2.cloned.1.call-start = ((), (), s32[]{:S(2)}) async-start(), calls=%async_computation.5 | async-start | bytes 4718592 | tf_op jit(solution)/shard_map/reduce_scatter | solution.py:340
  56.3 11.3 %collective-permute-start.7 = (bf16[128,512]{1,0:T(8,128)(2,1)S(1)}, bf16[128,512]{1,0:T(8,128)(2,1)S(1)}, u32[]{:S(2)}, u32[]{:S(2)}) collective-permute-start(bf16[128,512]{1,0:T(8,128)(2,1)S(1)} %collective-permute-done.3), channel_id=1, source_target_pairs={{0,2},{2,4},{4,6},{6,8},{8,10},{10,12},{12,14},{14,0},{1,3},{3,5},... | collective-permute-start | bytes 393224 | tf_op jit(solution)/shard_map/ppermute | solution.py:28
  58.2 11.2 %collective-permute-start.8 = (bf16[128,512]{1,0:T(8,128)(2,1)S(1)}, bf16[128,512]{1,0:T(8,128)(2,1)S(1)}, u32[]{:S(2)}, u32[]{:S(2)}) collective-permute-start(bf16[128,512]{1,0:T(8,128)(2,1)S(1)} %collective-permute-done.4), channel_id=1, source_target_pairs={{0,14},{2,0},{4,2},{6,4},{8,6},{10,8},{12,10},{14,12},{1,15},{3,1}... | collective-permute-start | bytes 393224 | tf_op jit(solution)/shard_map/ppermute | solution.py:28
  67.5 8.2 %collective-permute-start.9 = (bf16[64,512]{1,0:T(8,128)(2,1)S(1)}, bf16[64,512]{1,0:T(8,128)(2,1)S(1)}, u32[]{:S(2)}, u32[]{:S(2)}) collective-permute-start(bf16[64,512]{1,0:T(8,128)(2,1)S(1)} %slice.29), channel_id=1, source_target_pairs={{0,2},{2,4},{4,6},{6,8},{8,10},{10,12},{12,14},{14,0},{1,3},{3,5},... | collective-permute-start | bytes 196616 | tf_op jit(solution)/shard_map/ppermute | solution.py:28
  69.5 7.0 %collective-permute-start.10 = (bf16[64,512]{1,0:T(8,128)(2,1)S(1)}, bf16[64,512]{1,0:T(8,128)(2,1)S(1)}, u32[]{:S(2)}, u32[]{:S(2)}) collective-permute-start(bf16[64,512]{1,0:T(8,128)(2,1)S(1)} %slice.30), channel_id=1, source_target_pairs={{0,14},{2,0},{4,2},{6,4},{8,6},{10,8},{12,10},{14,12},{1,15},{3,1}... | collective-permute-start | bytes 196616 | tf_op jit(solution)/shard_map/ppermute | solution.py:28
  83.7 49.7 %collective-permute-start.13 = (bf16[2,1024,512]{2,1,0:T(8,128)(2,1)S(1)}, bf16[2,1024,512]{2,1,0:T(8,128)(2,1)}, u32[]{:S(2)}, u32[]{:S(2)}) collective-permute-start(bf16[2,1024,512]{2,1,0:T(8,128)(2,1)S(1)} %pad_maximum_fusion.rest_0_), channel_id=1, source_target_pairs={{0,32},{32,64},{64,96},{96,0},{1,33},{33,65},{65,97},{97,1},{2,34}... | collective-permute-start | bytes 6291464 | tf_op jit(solution)/shard_map/ppermute | solution.py:28
  87.0 50.7 %collective-permute-start.11 = (bf16[2,1024,512]{2,1,0:T(8,128)(2,1)S(1)}, bf16[2,1024,512]{2,1,0:T(8,128)(2,1)}, u32[]{:S(2)}, u32[]{:S(2)}) collective-permute-start(bf16[2,1024,512]{2,1,0:T(8,128)(2,1)S(1)} %pad_maximum_fusion.rest_0_), channel_id=1, source_target_pairs={{0,96},{32,0},{64,32},{96,64},{1,97},{33,1},{65,33},{97,65},{2,98}... | collective-permute-start | bytes 6291464 | tf_op jit(solution)/shard_map/ppermute | solution.py:28
  135.7 42.2 %collective-permute-start.14 = (bf16[1024,512]{1,0:T(8,128)(2,1)}, bf16[1024,512]{1,0:T(8,128)(2,1)S(1)}, u32[]{:S(2)}, u32[]{:S(2)}) collective-permute-start(bf16[1024,512]{1,0:T(8,128)(2,1)} %slice_bitcast_fusion), channel_id=1, source_target_pairs={{0,32},{32,64},{64,96},{96,0},{1,33},{33,65},{65,97},{97,1},{2,34}... | collective-permute-start | bytes 3145736 | tf_op jit(solution)/shard_map/ppermute | solution.py:28
  139.9 38.0 %collective-permute-start.12 = (bf16[1024,512]{1,0:T(8,128)(2,1)}, bf16[1024,512]{1,0:T(8,128)(2,1)}, u32[]{:S(2)}, u32[]{:S(2)}) collective-permute-start(bf16[1024,512]{1,0:T(8,128)(2,1)} %slice_bitcast_fusion.1), channel_id=1, source_target_pairs={{0,96},{32,0},{64,32},{96,64},{1,97},{33,1},{65,33},{97,65},{2,98}... | collective-permute-start | bytes 3145736 | tf_op jit(solution)/shard_map/ppermute | solution.py:28
  144.5 38.3 %collective-permute-start.15 = (bf16[2,1024,512]{2,1,0:T(8,128)(2,1)S(1)}, bf16[2,1024,512]{2,1,0:T(8,128)(2,1)}, u32[]{:S(2)}, u32[]{:S(2)}) collective-permute-start(bf16[2,1024,512]{2,1,0:T(8,128)(2,1)S(1)} %pad_maximum_fusion.rest_0_), channel_id=1, source_target_pairs={{0,16},{16,0},{1,17},{17,1},{2,18},{18,2},{3,19},{19,3},{4,20},{20... | collective-permute-start | bytes 6291464 | tf_op jit(solution)/shard_map/ppermute | solution.py:23
  148.7 36.7 %collective-permute-start.17 = (bf16[2,1024,512]{2,1,0:T(8,128)(2,1)}, bf16[2,1024,512]{2,1,0:T(8,128)(2,1)}, u32[]{:S(2)}, u32[]{:S(2)}) collective-permute-start(bf16[2,1024,512]{2,1,0:T(8,128)(2,1)} %collective-permute-done.13.rest_2_), channel_id=1, source_target_pairs={{0,16},{16,0},{1,17},{17,1},{2,18},{18,2},{3,19},{19,3},{4,20},{20... | collective-permute-start | bytes 6291464 | tf_op jit(solution)/shard_map/ppermute | solution.py:23
  150.6 34.8 %collective-permute-start.16 = (bf16[2,1024,512]{2,1,0:T(8,128)(2,1)}, bf16[2,1024,512]{2,1,0:T(8,128)(2,1)}, u32[]{:S(2)}, u32[]{:S(2)}) collective-permute-start(bf16[2,1024,512]{2,1,0:T(8,128)(2,1)} %collective-permute-done.11.rest_1_), channel_id=1, source_target_pairs={{0,16},{16,0},{1,17},{17,1},{2,18},{18,2},{3,19},{19,3},{4,20},{20... | collective-permute-start | bytes 6291464 | tf_op jit(solution)/shard_map/ppermute | solution.py:23
  177.9 5.4 %collective-permute-start.18 = (bf16[1024,512]{1,0:T(8,128)(2,1)}, bf16[1024,512]{1,0:T(8,128)(2,1)S(1)}, u32[]{:S(2)}, u32[]{:S(2)}) collective-permute-start(bf16[1024,512]{1,0:T(8,128)(2,1)} %collective-permute-done.12.rest_3_), channel_id=1, source_target_pairs={{0,16},{16,0},{1,17},{17,1},{2,18},{18,2},{3,19},{19,3},{4,20},{20... | collective-permute-start | bytes 3145736 | tf_op jit(solution)/shard_map/ppermute | solution.py:23
  207.8 4.8 %collective-permute-start.21 = (bf16[16,1024]{1,0:T(8,128)(2,1)S(1)}, bf16[16,1024]{1,0:T(8,128)(2,1)S(1)}, u32[]{:S(2)}, u32[]{:S(2)}) collective-permute-start(bf16[16,1024]{1,0:T(8,128)(2,1)S(1)} %get-tuple-element.27), channel_id=1, source_target_pairs={{128,0},{256,128},{384,256},{129,1},{257,129},{385,257},{130,2},{2... | collective-permute-start | bytes 98312 | tf_op jit(solution)/shard_map/ppermute | solution.py:334
  221.5 4.7 %collective-permute-start.22 = (bf16[16,1024]{1,0:T(8,128)(2,1)S(1)}, bf16[16,1024]{1,0:T(8,128)(2,1)S(1)}, u32[]{:S(2)}, u32[]{:S(2)}) collective-permute-start(bf16[16,1024]{1,0:T(8,128)(2,1)S(1)} %get-tuple-element.28), channel_id=1, source_target_pairs={{128,0},{256,128},{384,256},{129,1},{257,129},{385,257},{130,2},{2... | collective-permute-start | bytes 98312 | tf_op jit(solution)/shard_map/ppermute | solution.py:334
  (8 other events, 119.1 us)
Sparse Core Ops, SparseCore 0:
  10.1 72.1 all-gather.2
  85.0 45.7 all-gather.4
  260.4 55.1 reduce-scatter.1
